TPU v7x, 32 devices: a whole 2x2x4 slice. The times are simulated.
32 devices in a mesh: dp: 2 (over core), row: 4 (over y, x), col: 4 (over z).
Axes of the slice: x: 2, y: 2, z: 4, core: 2. Of those that a mesh axis runs over, the one named last changes fastest.
Arguments:
- block_input: float32 [1024, 1024], P(('dp', 'col'), 'row'), may hold values from -36 to 36
- out_cot: float32 [1024, 1024], P(('dp', 'col'), 'row'), may hold values from -6 to 6
- proj_weight: float32 [1024, 3, 1024], P('row', None, ('dp', 'col')), may hold values from -0.1875 to 0.1875
- conv_weight: float32 [3, 1024], P(None, ('dp', 'col')), may hold values from -3.5 to 3.5
- mixer_weight: float32 [1024, 1024], P(('dp', 'col'), 'row'), may hold values from -0.1875 to 0.1875
- up_weight: float32 [1024, 2, 4608], P('row', None, ('dp', 'col')), may hold values from -0.1875 to 0.1875
- down_weight: float32 [4608, 1024], P(('dp', 'col'), 'row'), may hold values from -0.09375 to 0.09375
- norm_gains: float32 [2, 1024], P(None, 'row'), may hold values from 0.25 to 1.75
- proj_moments: float32 [2, 1024, 3, 1024], P(None, 'row', None, ('dp', 'col')), may hold values from -1024 to 1024, as said below
- conv_moments: float32 [2, 3, 1024], P(None, None, ('dp', 'col')), may hold values from -1024 to 1024, as said below
- mixer_moments: float32 [2, 1024, 1024], P(None, ('dp', 'col'), 'row'), may hold values from -1024 to 1024, as said below
- up_moments: float32 [2, 1024, 2, 4608], P(None, 'row', None, ('dp', 'col')), may hold values from -1024 to 1024, as said below
- down_moments: float32 [2, 4608, 1024], P(None, ('dp', 'col'), 'row'), may hold values from -1024 to 1024, as said below
- gains_moments: float32 [2, 2, 1024], P(None, None, 'row'), may hold values from -1024 to 1024, as said below
Outputs:
- block_output: float32 [1024, 1024], P(('dp', 'col'), 'row')
- input_grad: float32 [1024, 1024], P(('dp', 'col'), 'row')
- proj_grad: float32 [1024, 3, 1024], P('row', None, ('dp', 'col'))
- conv_grad: float32 [3, 1024], P(None, ('dp', 'col'))
- mixer_grad: float32 [1024, 1024], P(('dp', 'col'), 'row')
- up_grad: float32 [1024, 2, 4608], P('row', None, ('dp', 'col'))
- down_grad: float32 [4608, 1024], P(('dp', 'col'), 'row')
- gains_grad: float32 [2, 1024], P(None, 'row')
- proj_new: float32 [1024, 3, 1024], P('row', None, ('dp', 'col'))
- conv_new: float32 [3, 1024], P(None, ('dp', 'col'))
- mixer_new: float32 [1024, 1024], P(('dp', 'col'), 'row')
- up_new: float32 [1024, 2, 4608], P('row', None, ('dp', 'col'))
- down_new: float32 [4608, 1024], P(('dp', 'col'), 'row')
- gains_new: float32 [2, 1024], P(None, 'row')
- proj_moments_new: float32 [2, 1024, 3, 1024], P(None, 'row', None, ('dp', 'col'))
- conv_moments_new: float32 [2, 3, 1024], P(None, None, ('dp', 'col'))
- mixer_moments_new: float32 [2, 1024, 1024], P(None, ('dp', 'col'), 'row')
- up_moments_new: float32 [2, 1024, 2, 4608], P(None, 'row', None, ('dp', 'col'))
- down_moments_new: float32 [2, 4608, 1024], P(None, ('dp', 'col'), 'row')
- gains_moments_new: float32 [2, 2, 1024], P(None, None, 'row')
Inputs may be any that keep to these rules, and one draw needn't show every extreme that they name: `proj_moments`: index 0 of the leading dimension holds first moments, index 1 second moments, which are positive. `conv_moments`: index 0 of the leading dimension holds first moments, index 1 second moments, which are positive. `mixer_moments`: index 0 of the leading dimension holds first moments, index 1 second moments, which are positive. `up_moments`: index 0 of the leading dimension holds first moments, index 1 second moments, which are positive. `down_moments`: index 0 of the leading dimension holds first moments, index 1 second moments, which are positive. `gains_moments`: index 0 of the leading dimension holds first moments, index 1 second moments, which are positive.
All inputs are finite; a program needn't handle non-finite values.
Results may differ from a plain program's by a relative error of at most 0.012.
The roundings to bfloat16 on the way count: a program that leaves them out, or rounds other values in their place, can miss the bound.
Values may be sent and summed in bfloat16 or wider, within the bound.
A program may use at most 128 MiB of HBM per device.

v0:
```python
import jax
import jax.numpy as jnp
from jax import lax
from jax.sharding import PartitionSpec as P

D = 1024
KERNEL = 3
STEP = 4


eps_norm = 1e-05
beta_first = 0.9
beta_second = 0.999
eps_adam = 1e-08
matrix_rate = 0.01
small_rate = 0.1
decay_rate = 0.1


def shifted(x, axis, by):
    devices = lax.axis_size(axis)
    pairs = [(i, i + by) for i in range(devices) if 0 <= i + by < devices]
    return lax.ppermute(x, axis, pairs)


def plain_product(left_side, right_side):
    return jnp.dot(left_side, right_side, preferred_element_type=jnp.float32)


def contract_rows(left_side, right_side):
    return lax.dot_general(
        left_side, right_side, (((0,), (0,)), ((), ())), preferred_element_type=jnp.float32
    )


def contract_cols(left_side, right_side):
    return lax.dot_general(
        left_side, right_side, (((1,), (1,)), ((), ())), preferred_element_type=jnp.float32
    )


def adam_step(parameter, gradient, moments, step_rate, decay_weight):
    first_moment = beta_first * moments[0] + (1.0 - beta_first) * gradient
    second_moment = beta_second * moments[1] + (1.0 - beta_second) * gradient * gradient
    first_hat = first_moment / (1.0 - beta_first**STEP)
    second_hat = second_moment / (1.0 - beta_second**STEP)
    update = first_hat / (jnp.sqrt(second_hat) + eps_adam) + decay_weight * parameter
    return (parameter - step_rate * update, jnp.stack([first_moment, second_moment]))


def width_total(row_values):
    return lax.psum(row_values, "row")


def token_gather(row_values):
    return lax.all_gather(row_values, "col", axis=0, tiled=True)


def hidden_gather(row_values):
    return lax.all_gather(row_values, "row", axis=0, tiled=True)


def row_reduce(left_side, right_side, transposed):

    def row_partial_term():
        if transposed:
            return contract_cols(left_side, right_side)
        return plain_product(left_side, right_side)

    return lax.psum_scatter(row_partial_term(), "row", scatter_dimension=0, tiled=True)


def row_product(left_side, right_side, transposed):
    return row_reduce(left_side, right_side, transposed)


def col_reduce(left_side, right_side, transposed):

    def col_partial_term():
        if transposed:
            return contract_cols(left_side, right_side)
        return plain_product(left_side, right_side)

    return lax.psum_scatter(col_partial_term(), "col", scatter_dimension=0, tiled=True)


def inverse_rms(residual):
    row_total = width_total(jnp.sum(residual * residual, axis=1))
    return lax.rsqrt(row_total / D + eps_norm)[:, None]


def norm_back(residual, inverse, gain_row, d_normed):
    scaled = d_normed * gain_row
    row_total = width_total(jnp.sum(scaled * residual, axis=1))[:, None] / D
    d_residual = inverse * (scaled - residual * inverse * inverse * row_total)
    gain_part = jnp.sum(d_normed * residual * inverse, axis=0)
    return (d_residual, gain_part)


def on_device(
    block_input,
    out_cot,
    proj_weight,
    conv_weight,
    mixer_weight,
    up_weight,
    down_weight,
    norm_gains,
    proj_moments,
    conv_moments,
    mixer_moments,
    up_moments,
    down_moments,
    gains_moments,
):
    wide_proj, conv_low, wide_mixer, wide_up, wide_down = (
        lax.all_gather(proj_weight.astype(jnp.bfloat16), "dp", axis=2, tiled=True),
        lax.all_gather(conv_weight.astype(jnp.bfloat16), "dp", axis=1, tiled=True),
        lax.all_gather(mixer_weight.astype(jnp.bfloat16), "dp", axis=0, tiled=True),
        lax.all_gather(up_weight.astype(jnp.bfloat16), "dp", axis=2, tiled=True),
        lax.all_gather(down_weight.astype(jnp.bfloat16), "dp", axis=0, tiled=True),
    )
    width_local = wide_proj.shape[0]
    channels = wide_proj.shape[2]
    units = wide_up.shape[2]
    proj_matrix = wide_proj.reshape(width_local, 3 * channels)
    up_matrix = wide_up.reshape(width_local, 2 * units)
    conv_taps = conv_low.astype(jnp.float32)
    gain_one = norm_gains[0]
    gain_two = norm_gains[1]
    history = KERNEL - 1
    inverse_one = inverse_rms(block_input)
    normed_one = (block_input * inverse_one * gain_one).astype(jnp.bfloat16)
    gathered_one = token_gather(normed_one)
    inner_rows = gathered_one.shape[0] // lax.axis_size("row")
    projected = row_product(gathered_one, proj_matrix, False)
    gate_b = projected[:, :channels]
    gate_c = projected[:, channels : 2 * channels]
    values_x = projected[:, 2 * channels :]
    mixed_input = gate_b * values_x
    left_rim = shifted(mixed_input[inner_rows - history :], "row", 1)
    padded = jnp.concatenate([left_rim, mixed_input], axis=0)
    convolved = conv_taps[0] * padded[0:inner_rows]
    for offset in range(1, KERNEL):
        convolved = convolved + conv_taps[offset] * padded[offset : offset + inner_rows]
    gated = (gate_c * convolved).astype(jnp.bfloat16)
    gathered_gated = hidden_gather(gated)
    mixer_out = col_reduce(gathered_gated, wide_mixer, False)
    residual_two = block_input + mixer_out
    inverse_two = inverse_rms(residual_two)
    normed_two = (residual_two * inverse_two * gain_two).astype(jnp.bfloat16)
    gathered_two = token_gather(normed_two)
    gate_up = lax.psum_scatter(
        plain_product(gathered_two, up_matrix), "row", scatter_dimension=0, tiled=True
    )
    gate_pre = gate_up[:, :units]
    lifted = gate_up[:, units:]
    sigmoid_gate = jax.nn.sigmoid(gate_pre)
    swish_gate = gate_pre * sigmoid_gate
    hidden = (swish_gate * lifted).astype(jnp.bfloat16)
    gathered_hidden = hidden_gather(hidden)
    ffn_out = col_reduce(gathered_hidden, wide_down, False)
    block_output = residual_two + ffn_out
    gathered_cot = token_gather(out_cot.astype(jnp.bfloat16))
    d_hidden = row_product(gathered_cot, wide_down, True)
    d_gate = d_hidden * lifted * sigmoid_gate * (1.0 + gate_pre * (1.0 - sigmoid_gate))
    d_lifted = d_hidden * swish_gate
    d_gate_up = jnp.concatenate([d_gate, d_lifted], axis=1).astype(jnp.bfloat16)
    down_part = contract_rows(gathered_hidden, gathered_cot)
    gathered_dgate = hidden_gather(d_gate_up)
    up_part = contract_rows(gathered_two, gathered_dgate)
    d_normed_two = col_reduce(gathered_dgate, up_matrix, True)
    d_norm_two, gain_two_part = norm_back(residual_two, inverse_two, gain_two, d_normed_two)
    d_residual = out_cot + d_norm_two
    gathered_dres = token_gather(d_residual.astype(jnp.bfloat16))
    d_gated = row_product(gathered_dres, wide_mixer, True)
    mixer_part = contract_rows(gathered_gated, gathered_dres)
    d_convolved = d_gated * gate_c
    d_gate_c = d_gated * convolved
    next_rim = shifted(d_convolved[:history], "row", -1)
    extended = jnp.concatenate([d_convolved, next_rim], axis=0)
    d_mixed = conv_taps[history] * extended[0:inner_rows]
    for offset in range(1, KERNEL):
        d_mixed = d_mixed + conv_taps[history - offset] * extended[offset : offset + inner_rows]
    conv_part = jnp.stack(
        [
            jnp.sum(d_convolved * padded[offset : offset + inner_rows], axis=0)
            for offset in range(KERNEL)
        ]
    )
    d_projected = jnp.concatenate([d_mixed * values_x, d_gate_c, d_mixed * gate_b], axis=1).astype(
        jnp.bfloat16
    )
    gathered_dproj = hidden_gather(d_projected)
    proj_part = contract_rows(gathered_one, gathered_dproj)
    d_normed_one = col_reduce(gathered_dproj, proj_matrix, True)
    d_norm_one, gain_one_part = norm_back(block_input, inverse_one, gain_one, d_normed_one)
    input_grad = d_residual + d_norm_one
    proj_grad, mixer_grad, up_grad, down_grad = (
        lax.psum_scatter(
            proj_part.reshape(width_local, 3, channels), "dp", scatter_dimension=2, tiled=True
        ),
        lax.psum_scatter(mixer_part, "dp", scatter_dimension=0, tiled=True),
        lax.psum_scatter(
            up_part.reshape(width_local, 2, units), "dp", scatter_dimension=2, tiled=True
        ),
        lax.psum_scatter(down_part, "dp", scatter_dimension=0, tiled=True),
    )
    conv_total = lax.psum(conv_part, ("dp", "row"))
    shard_width = conv_weight.shape[1]
    conv_grad = lax.dynamic_slice_in_dim(
        conv_total, lax.axis_index("dp") * shard_width, shard_width, 1
    )
    gains_grad = lax.psum(jnp.stack([gain_one_part, gain_two_part]), ("dp", "col"))
    proj_new, proj_moments_new = adam_step(
        proj_weight, proj_grad, proj_moments, matrix_rate, decay_rate
    )
    conv_new, conv_moments_new = adam_step(conv_weight, conv_grad, conv_moments, small_rate, 0.0)
    mixer_new, mixer_moments_new = adam_step(
        mixer_weight, mixer_grad, mixer_moments, matrix_rate, decay_rate
    )
    up_new, up_moments_new = adam_step(up_weight, up_grad, up_moments, matrix_rate, decay_rate)
    down_new, down_moments_new = adam_step(
        down_weight, down_grad, down_moments, matrix_rate, decay_rate
    )
    gains_new, gains_moments_new = adam_step(norm_gains, gains_grad, gains_moments, small_rate, 0.0)
    return (
        block_output,
        input_grad,
        proj_grad,
        conv_grad,
        mixer_grad,
        up_grad,
        down_grad,
        gains_grad,
        proj_new,
        conv_new,
        mixer_new,
        up_new,
        down_new,
        gains_new,
        proj_moments_new,
        conv_moments_new,
        mixer_moments_new,
        up_moments_new,
        down_moments_new,
        gains_moments_new,
    )


def solution(mesh):
    in_specs = (
        P(("dp", "col"), "row"),
        P(("dp", "col"), "row"),
        P("row", None, ("dp", "col")),
        P(None, ("dp", "col")),
        P(("dp", "col"), "row"),
        P("row", None, ("dp", "col")),
        P(("dp", "col"), "row"),
        P(None, "row"),
        P(None, "row", None, ("dp", "col")),
        P(None, None, ("dp", "col")),
        P(None, ("dp", "col"), "row"),
        P(None, "row", None, ("dp", "col")),
        P(None, ("dp", "col"), "row"),
        P(None, None, "row"),
    )
    out_specs = (
        P(("dp", "col"), "row"),
        P(("dp", "col"), "row"),
        P("row", None, ("dp", "col")),
        P(None, ("dp", "col")),
        P(("dp", "col"), "row"),
        P("row", None, ("dp", "col")),
        P(("dp", "col"), "row"),
        P(None, "row"),
        P("row", None, ("dp", "col")),
        P(None, ("dp", "col")),
        P(("dp", "col"), "row"),
        P("row", None, ("dp", "col")),
        P(("dp", "col"), "row"),
        P(None, "row"),
        P(None, "row", None, ("dp", "col")),
        P(None, None, ("dp", "col")),
        P(None, ("dp", "col"), "row"),
        P(None, "row", None, ("dp", "col")),
        P(None, ("dp", "col"), "row"),
        P(None, None, "row"),
    )
    return jax.shard_map(
        on_device, mesh=mesh, in_specs=in_specs, out_specs=out_specs, check_vma=False
    )
```

profile of v0, /device:TPU:0, one launch (start us, length us, event | category | flops | bytes accessed | tf_op | source)
XLA Modules:
  0.0 473.4 jit_solution(9313080685779793156)
XLA Ops:
  8.8 1.0 multiply_reduce_fusion.8
  9.8 11.4 %psum.42 = f32[128]{0:T(128)S(1)} all-reduce(f32[128]{0:T(128)S(1)} %multiply_reduce_fusion.8), channel_id=1, replica_groups=mesh['dp'=2,'row'=4,'col'=4] {'row'}, use_global_device_ids=true, to_apply=%region_1.0 | all-reduce | flops 128 | bytes 1024 | tf_op jit(solution)/shard_map/psum | solution.py:52
  21.2 1.0 multiply_convert_fusion.8
  22.3 14.6 %all_gather.39 = bf16[512,256]{1,0:T(8,128)(2,1)S(1)} all-gather(bf16[128,256]{1,0:T(8,128)(2,1)S(1)} %multiply_convert_fusion.8), channel_id=1, replica_groups=mesh['dp'=2,'row'=4,'col'=4] {'col'}, dimensions={0}, use_global_device_ids=true | all-gather | bytes 327680 | tf_op jit(solution)/shard_map/all_gather | solution.py:56
  36.9 1.3 copy.39
  38.2 2.1 all_gather.40
  40.3 1.5 fusion.34
  42.8 1.8 all_gather.41
  44.6 27.2 %reduce-scatter.13.cloned.1.call-done = f32[128,768]{1,0:T(8,128)} async-done(((f32[512,768]{1,0:T(8,128)}), f32[128,768]{1,0:T(8,128)}) %reduce-scatter.13.cloned.1.call-update) | async-done | bytes 393232 | tf_op jit(solution)/shard_map/reduce_scatter | solution.py:70
  71.8 1.0 slice_multiply_fusion
  72.8 3.5 collective-permute-start
  76.3 1.9 all_gather.43
  78.2 1.7 multiply_convert_fusion.7
  79.9 10.3 %all_gather.42 = bf16[512,256]{1,0:T(8,128)(2,1)S(1)} all-gather(bf16[128,256]{1,0:T(8,128)(2,1)S(1)} %get-tuple-element.56), channel_id=1, replica_groups=mesh['dp'=2,'row'=4,'col'=4] {'row'}, dimensions={0}, use_global_device_ids=true | all-gather | bytes 327680 | tf_op jit(solution)/shard_map/all_gather | solution.py:60
  90.9 1.0 fusion.35
  92.1 0.9 convert_element_type.45
  93.9 15.3 %all_gather.48 = bf16[512,256]{1,0:T(8,128)(2,1)S(1)} all-gather(bf16[128,256]{1,0:T(8,128)(2,1)S(1)} %convert_element_type.48), channel_id=1, replica_groups=mesh['dp'=2,'row'=4,'col'=4] {'col'}, dimensions={0}, use_global_device_ids=true | all-gather | bytes 327680 | tf_op jit(solution)/shard_map/all_gather | solution.py:56
  109.2 2.2 all_gather.47
  111.4 1.9 fusion.38
  114.3 1.0 multiply_reduce_fusion.7
  115.3 9.6 %psum.43 = f32[128]{0:T(128)S(1)} all-reduce(f32[128]{0:T(128)S(1)} %get-tuple-element.54), channel_id=1, replica_groups=mesh['dp'=2,'row'=4,'col'=4] {'row'}, use_global_device_ids=true, to_apply=%region_5.0 | all-reduce | flops 128 | bytes 1024 | tf_op jit(solution)/shard_map/psum | solution.py:52
  125.1 14.5 %all_gather.44 = bf16[512,256]{1,0:T(8,128)(2,1)S(1)} all-gather(bf16[128,256]{1,0:T(8,128)(2,1)S(1)} %multiply_convert_fusion.6), channel_id=1, replica_groups=mesh['dp'=2,'row'=4,'col'=4] {'col'}, dimensions={0}, use_global_device_ids=true | all-gather | bytes 327680 | tf_op jit(solution)/shard_map/all_gather | solution.py:56
  139.5 4.3 fusion.36
  143.9 11.1 %reduce-scatter.21.cloned.1.call-done = f32[128,1152]{1,0:T(8,128)} async-done(((f32[512,1152]{1,0:T(8,128)}), f32[128,1152]{1,0:T(8,128)}) %reduce-scatter.21.cloned.1.call-update) | async-done | bytes 589840 | tf_op jit(solution)/shard_map/reduce_scatter | solution.py:70
  155.0 59.9 %reduce-scatter.17.cloned.1.call-done = f32[128,2304]{1,0:T(8,128)} async-done(((f32[512,2304]{1,0:T(8,128)}), f32[128,2304]{1,0:T(8,128)}) %reduce-scatter.17.cloned.1.call-update) | async-done | bytes 1179664 | tf_op jit(solution)/shard_map/reduce_scatter | solution.py:153
  214.8 2.5 multiply_convert_fusion.1
  217.3 0.9 pad_maximum_fusion.3
  218.8 36.9 %all-gather.8.cloned.1.call-done = bf16[512,2304]{1,0:T(8,128)(2,1)} async-done(((bf16[128,2304]{1,0:T(8,128)(2,1)}), bf16[512,2304]{1,0:T(8,128)(2,1)}) %all-gather.8.cloned.1.call-update) | async-done | bytes 2359312 | tf_op jit(solution)/shard_map/all_gather | solution.py:60
  255.7 3.5 fusion.39
  259.3 26.3 %all-gather.6.cloned.1.call-done = bf16[512,1152]{1,0:T(8,128)(2,1)} async-done(((bf16[128,1152]{1,0:T(8,128)(2,1)}), bf16[512,1152]{1,0:T(8,128)(2,1)}) %all-gather.6.cloned.1.call-update) | async-done | bytes 1179664 | tf_op jit(solution)/shard_map/all_gather | solution.py:60
  285.6 2.6 fusion.37
  288.2 22.1 %reduce-scatter.23.cloned.1.call-done = f32[128,256]{1,0:T(8,128)} async-done(((f32[512,256]{1,0:T(8,128)}), f32[128,256]{1,0:T(8,128)}) %reduce-scatter.23.cloned.1.call-update) | async-done | bytes 131088 | tf_op jit(solution)/shard_map/reduce_scatter | solution.py:84
  310.3 1.6 multiply_reduce_fusion
  311.9 9.8 %psum.44 = f32[128]{0:T(128)S(1)} all-reduce(f32[128]{0:T(128)S(1)} %get-tuple-element.45), channel_id=1, replica_groups=mesh['dp'=2,'row'=4,'col'=4] {'row'}, use_global_device_ids=true, to_apply=%region_11.0 | all-reduce | flops 128 | bytes 1024 | tf_op jit(solution)/shard_map/psum | solution.py:52
  322.2 11.1 %reduce-scatter.19.cloned.1.call-done = f32[128,256]{1,0:T(8,128)} async-done(((f32[512,256]{1,0:T(8,128)}), f32[128,256]{1,0:T(8,128)}) %reduce-scatter.19.cloned.1.call-update) | async-done | bytes 131088 | tf_op jit(solution)/shard_map/reduce_scatter | solution.py:84
  333.3 1.9 fusion.29
  335.2 13.9 %all_gather.50 = bf16[512,256]{1,0:T(8,128)(2,1)S(1)} all-gather(bf16[128,256]{1,0:T(8,128)(2,1)S(1)} %get-tuple-element.52), channel_id=1, replica_groups=mesh['dp'=2,'row'=4,'col'=4] {'col'}, dimensions={0}, use_global_device_ids=true | all-gather | bytes 327680 | tf_op jit(solution)/shard_map/all_gather | solution.py:56
  349.7 2.0 fusion.40
  351.8 2.5 fusion.45
  354.3 20.7 %reduce-scatter.25.cloned.1.call-done = f32[128,256]{1,0:T(8,128)} async-done(((f32[512,256]{1,0:T(8,128)}), f32[128,256]{1,0:T(8,128)}) %reduce-scatter.25.cloned.1.call-update) | async-done | bytes 131088 | tf_op jit(solution)/shard_map/reduce_scatter | solution.py:70
  375.1 2.3 multiply_reduce_fusion.4
  377.3 1.3 collective-permute-start.1
  378.6 1.0 fusion.43
  379.7 3.2 collective-permute-done.1
  383.7 0.9 pad_maximum_fusion.5
  384.6 13.0 %all_gather.51 = bf16[512,768]{1,0:T(8,128)(2,1)S(1)} all-gather(bf16[128,768]{1,0:T(8,128)(2,1)S(1)} %pad_maximum_fusion.5), channel_id=1, replica_groups=mesh['dp'=2,'row'=4,'col'=4] {'row'}, dimensions={0}, use_global_device_ids=true | all-gather | bytes 983040 | tf_op jit(solution)/shard_map/all_gather | solution.py:60
  397.6 1.2 fusion.41
  398.9 1.3 fusion.42
  400.3 4.1 fusion.44
  404.4 1.2 fusion.30
  406.7 2.7 fusion.6
  409.4 1.1 pad_maximum_fusion.1
  410.6 1.7 fusion.17
  413.0 13.8 %psum.46 = f32[3,256]{1,0:T(4,128)S(1)} all-reduce(f32[3,256]{1,0:T(4,128)S(1)} %pad_maximum_fusion.8), channel_id=1, replica_groups=mesh['dp'=2,'row'=4,'col'=4] {'dp','row'}, use_global_device_ids=true, to_apply=%region_20.0 | all-reduce | flops 768 | bytes 6144 | tf_op jit(solution)/shard_map/psum | solution.py:209
  428.0 1.0 multiply_reduce_fusion.1
  429.1 9.3 %psum.45 = f32[128]{0:T(128)S(1)} all-reduce(f32[128]{0:T(128)S(1)} %get-tuple-element.43), channel_id=1, replica_groups=mesh['dp'=2,'row'=4,'col'=4] {'row'}, use_global_device_ids=true, to_apply=%region_15.0 | all-reduce | flops 128 | bytes 1024 | tf_op jit(solution)/shard_map/psum | solution.py:52
  438.4 15.2 %psum.47 = f32[2,256]{1,0:T(2,128)S(1)} all-reduce(f32[2,256]{1,0:T(2,128)S(1)} %pad_maximum_fusion.11), channel_id=1, replica_groups=mesh['dp'=2,'row'=4,'col'=4] {'dp','col'}, use_global_device_ids=true, to_apply=%region_26.0 | all-reduce | flops 512 | bytes 4096 | tf_op jit(solution)/shard_map/psum | solution.py:214
  454.8 1.7 multiply_add_fusion
  456.5 1.3 fusion.14
  457.9 1.1 copy.50
  459.0 0.9 copy.49
  459.9 0.9 copy.48
  460.9 3.9 fusion.4
  464.7 1.6 pad_maximum_fusion
  (147 shorter events, 12.0 us)
Async XLA Ops:
  8.0 63.8 %reduce-scatter.13.cloned.1.call-start = ((), (), s32[]{:S(2)}) async-start(), calls=%async_computation.12 | async-start | bytes 1966080 | tf_op jit(solution)/shard_map/reduce_scatter | solution.py:70
  21.2 1.0 copy-start.31
  36.9 4.9 %copy-start.3 = (bf16[512,256]{1,0:T(8,128)(2,1)}, bf16[512,256]{1,0:T(8,128)(2,1)S(1)}, u32[]{:S(2)}) copy-start(bf16[512,256]{1,0:T(8,128)(2,1)S(1)} %all_gather.39) | copy-start | bytes 786436
  41.8 0.7 copy-start.28
  41.8 0.9 copy-start.18
  41.9 72.2 %reduce-scatter.15.cloned.1.call-start = ((), (), s32[]{:S(2)}) async-start(), calls=%async_computation.13 | async-start | bytes 655360 | tf_op jit(solution)/shard_map/reduce_scatter | solution.py:84
  44.6 47.4 %copy-start.23 = (f32[1,256]{1,0:T(1,128)}, f32[1,256]{1,0:T(1,128)S(1)}, u32[]{:S(2)}) copy-start(f32[1,256]{1,0:T(1,128)S(1)} %get-tuple-element.88) | copy-start | bytes 3076
  72.8 19.2 %copy-start.15 = (f32[128,256]{1,0:T(8,128)}, f32[128,256]{1,0:T(8,128)S(1)}, u32[]{:S(2)}) copy-start(f32[128,256]{1,0:T(8,128)S(1)} %slice_multiply_fusion) | copy-start | bytes 393220
  72.8 19.2 %copy-start.1 = (f32[256,2,576]{0,2,1:T(8,128)S(1)}, f32[256,2,576]{0,2,1:T(8,128)}, u32[]{:S(2)}) copy-start(f32[256,2,576]{0,2,1:T(8,128)} %param.19) | copy-start | bytes 3538948
  72.8 5.4 %collective-permute-start = (f32[2,256]{1,0:T(2,128)S(1)}, f32[2,256]{1,0:T(2,128)S(1)}, u32[]{:S(2)}, u32[]{:S(2)}) collective-permute-start(f32[2,256]{1,0:T(2,128)S(1)} %slice.121), channel_id=1, source_target_pairs={{0,4},{4,8},{8,12},{1,5},{5,9},{9,13},{2,6},{6,10},{10,14},{3,7},{... | collective-permute-start | bytes 6152 | tf_op jit(solution)/shard_map/ppermute | solution.py:23
  78.2 12.0 %copy-start.17 = (bf16[256,256]{1,0:T(8,128)(2,1)}, bf16[256,256]{1,0:T(8,128)(2,1)S(1)}, u32[]{:S(2)}) copy-start(bf16[256,256]{1,0:T(8,128)(2,1)S(1)} %all_gather.43) | copy-start | bytes 393220
  78.2 1.7 copy-start.25
  90.2 0.7 copy-start.5
  92.0 1.1 copy-start.10
  92.0 47.5 %all-gather.4.cloned.1.call-start = ((), (), s32[]{:S(2)}) async-start(), calls=%async_computation.14 | async-start | bytes 1769472 | tf_op jit(solution)/shard_map/all_gather | solution.py:120
  92.9 0.9 copy-start.20
  93.0 62.0 %reduce-scatter.21.cloned.1.call-start = ((), (), s32[]{:S(2)}) async-start(), calls=%async_computation.18 | async-start | bytes 2949120 | tf_op jit(solution)/shard_map/reduce_scatter | solution.py:70
  109.2 2.2 copy-start.7
  113.4 0.9 copy-start.2
  113.4 101.4 %reduce-scatter.17.cloned.1.call-start = ((), (), s32[]{:S(2)}) async-start(), calls=%async_computation.15 | async-start | bytes 5898240 | tf_op jit(solution)/shard_map/reduce_scatter | solution.py:153
  115.3 195.0 %copy-start.12 = (f32[128,256]{1,0:T(8,128)}, f32[128,256]{1,0:T(8,128)S(1)}, u32[]{:S(2)}) copy-start(f32[128,256]{1,0:T(8,128)S(1)} %get-tuple-element.55) | copy-start | bytes 393220
  125.0 185.3 %copy-start.33 = (f32[128]{0:T(128)}, f32[128]{0:T(128)S(1)}, u32[]{:S(2)}) copy-start(f32[128]{0:T(128)S(1)} %add_rsqrt_fusion) | copy-start | bytes 1540
  143.8 111.9 %all-gather.8.cloned.1.call-start = ((), (), s32[]{:S(2)}) async-start(), calls=%async_computation.19 | async-start | bytes 2949120 | tf_op jit(solution)/shard_map/all_gather | solution.py:60
  218.2 67.4 %all-gather.6.cloned.1.call-start = ((), (), s32[]{:S(2)}) async-start(), calls=%async_computation.16 | async-start | bytes 1474560 | tf_op jit(solution)/shard_map/all_gather | solution.py:60
  218.8 91.5 %reduce-scatter.23.cloned.1.call-start = ((), (), s32[]{:S(2)}) async-start(), calls=%async_computation.20 | async-start | bytes 655360 | tf_op jit(solution)/shard_map/reduce_scatter | solution.py:84
  259.3 74.0 %reduce-scatter.19.cloned.1.call-start = ((), (), s32[]{:S(2)}) async-start(), calls=%async_computation.17 | async-start | bytes 655360 | tf_op jit(solution)/shard_map/reduce_scatter | solution.py:84
  288.2 86.9 %reduce-scatter.25.cloned.1.call-start = ((), (), s32[]{:S(2)}) async-start(), calls=%async_computation.21 | async-start | bytes 655360 | tf_op jit(solution)/shard_map/reduce_scatter | solution.py:70
  322.1 29.6 %copy-start = (bf16[512,1152]{1,0:T(8,128)(2,1)S(1)}, bf16[512,1152]{1,0:T(8,128)(2,1)}, u32[]{:S(2)}) copy-start(bf16[512,1152]{1,0:T(8,128)(2,1)} %all-gather.6.cloned.1.call-done) | copy-start | bytes 3538948
  349.0 0.7 copy-start.8
  351.7 54.6 %reduce-scatter.35.cloned.1.call-start = ((), (), s32[]{:S(2)}) async-start(), calls=%async_computation.26 | async-start | bytes 1769472 | tf_op jit(solution)/shard_map/reduce_scatter | solution.py:207
  354.2 20.8 %copy-start.13 = (f32[128,768]{1,0:T(8,128)S(1)}, f32[128,768]{1,0:T(8,128)}, u32[]{:S(2)}) copy-start(f32[128,768]{1,0:T(8,128)} %reduce-scatter.13.cloned.1.call-done) | copy-start | bytes 1179652
  354.2 20.8 %copy-start.16 = (f32[128,256]{1,0:T(8,128)S(1)}, f32[128,256]{1,0:T(8,128)}, u32[]{:S(2)}) copy-start(f32[128,256]{1,0:T(8,128)} %copy-done.15) | copy-start | bytes 393220
  354.2 24.4 %copy-start.6 = (bf16[512,256]{1,0:T(8,128)(2,1)S(1)}, bf16[512,256]{1,0:T(8,128)(2,1)}, u32[]{:S(2)}) copy-start(bf16[512,256]{1,0:T(8,128)(2,1)} %copy-done.5) | copy-start | bytes 786436
  354.2 24.4 %copy-start.9 = (bf16[512,256]{1,0:T(8,128)(2,1)S(1)}, bf16[512,256]{1,0:T(8,128)(2,1)}, u32[]{:S(2)}) copy-start(bf16[512,256]{1,0:T(8,128)(2,1)} %copy-done.8) | copy-start | bytes 786436
  354.3 28.6 %copy-start.24 = (f32[1,256]{1,0:T(1,128)S(1)}, f32[1,256]{1,0:T(1,128)}, u32[]{:S(2)}) copy-start(f32[1,256]{1,0:T(1,128)} %copy-done.23) | copy-start | bytes 3076
  354.3 56.2 %reduce-scatter.31.cloned.1.call-start = ((), (), s32[]{:S(2)}) async-start(), calls=%async_computation.24 | async-start | bytes 393216 | tf_op jit(solution)/shard_map/reduce_scatter | solution.py:203
  377.3 5.6 %collective-permute-start.1 = (f32[2,256]{1,0:T(2,128)S(1)}, f32[2,256]{1,0:T(2,128)}, u32[]{:S(2)}, u32[]{:S(2)}) collective-permute-start(f32[2,256]{1,0:T(2,128)S(1)} %slice.128), channel_id=1, source_target_pairs={{4,0},{8,4},{12,8},{5,1},{9,5},{13,9},{6,2},{10,6},{14,10},{7,3},{... | collective-permute-start | bytes 6152 | tf_op jit(solution)/shard_map/ppermute | solution.py:23
  379.6 48.4 %reduce-scatter.27.cloned.1.call-start = ((), (), s32[]{:S(2)}) async-start(), calls=%async_computation.22 | async-start | bytes 655360 | tf_op jit(solution)/shard_map/reduce_scatter | solution.py:84
  397.6 1.2 copy-start.4
  398.8 57.7 %reduce-scatter.29.cloned.1.call-start = ((), (), s32[]{:S(2)}) async-start(), calls=%async_computation.23 | async-start | bytes 1179648 | tf_op jit(solution)/shard_map/reduce_scatter | solution.py:200
  400.2 60.6 %reduce-scatter.33.cloned.1.call-start = ((), (), s32[]{:S(2)}) async-start(), calls=%async_computation.25 | async-start | bytes 3538944 | tf_op jit(solution)/shard_map/reduce_scatter | solution.py:204
  405.6 0.7 copy-start.39
  405.6 1.1 copy-start.11
  409.3 1.2 copy-start.19
  409.3 1.2 copy-start.22
  410.4 2.6 copy-start.34
  410.4 2.6 copy-start.35
  410.4 2.6 copy-start.36
  410.4 16.4 %copy-start.29 = (f32[3,128]{1,0:T(4,128)S(1)}, f32[3,128]{1,0:T(4,128)}, u32[]{:S(2)}) copy-start(f32[3,128]{1,0:T(4,128)} %param.17) | copy-start | bytes 4612
  410.5 17.6 %copy-start.32 = (f32[128]{0:T(128)S(1)}, f32[128]{0:T(128)}, u32[]{:S(2)}) copy-start(f32[128]{0:T(128)} %copy-done.31) | copy-start | bytes 1540
  410.5 27.9 %copy-start.37 = (f32[256]{0:T(256)S(1)}, f32[256]{0:T(256)}, u32[]{:S(2)}) copy-start(f32[256]{0:T(256)} %get-tuple-element.44) | copy-start | bytes 3076
  410.5 43.1 %copy-start.26 = (f32[2,256]{1,0:T(2,128)S(1)}, f32[2,256]{1,0:T(2,128)}, u32[]{:S(2)}) copy-start(f32[2,256]{1,0:T(2,128)} %param.21) | copy-start | bytes 6148
  410.5 43.1 %copy-start.38 = (f32[2,2,256]{2,1,0:T(2,128)S(1)}, f32[2,2,256]{2,1,0:T(2,128)}, u32[]{:S(2)}) copy-start(f32[2,2,256]{2,1,0:T(2,128)} %param.27) | copy-start | bytes 12292
  410.5 44.3 %copy-start.21 = (f32[128,256]{1,0:T(8,128)S(1)}, f32[128,256]{1,0:T(8,128)}, u32[]{:S(2)}) copy-start(f32[128,256]{1,0:T(8,128)} %get-tuple-element.53) | copy-start | bytes 393220
  426.8 31.0 %copy-start.30 = (f32[3,128]{1,0:T(4,128)}, f32[3,128]{1,0:T(4,128)S(1)}, u32[]{:S(2)}) copy-start(f32[3,128]{1,0:T(4,128)S(1)} %get-tuple-element.48) | copy-start | bytes 4612
  453.6 4.2 copy-start.27
  457.9 2.1 copy-start.14
Sparse Core Ops, SparseCore 0:
  42.0 29.7 reduce-scatter.12
  92.1 21.8 reduce-scatter.14
  117.6 37.2 reduce-scatter.20
  157.8 56.9 reduce-scatter.16
  218.3 37.3 all-gather.7
  257.9 27.5 all-gather.5
  288.4 21.8 reduce-scatter.22
  313.1 20.1 reduce-scatter.18
  351.8 23.1 reduce-scatter.24
  378.3 8.5 reduce-scatter.34
  390.2 9.0 reduce-scatter.30
  402.0 22.9 reduce-scatter.26
  427.8 6.3 reduce-scatter.28
  437.5 11.1 reduce-scatter.32
Sparse Core Ops, SparseCore 1:
  94.6 9.1 all-gather.3
where the time goes:
time: 476 us; the launch traced here: 473 us
  waiting for transfers between devices  220 us (46%)
  blocking collectives  159 us (33%)
  other arithmetic  35.6 us (7%)
  matrix products  26.9 us (6%)
  between operations  15.8 us (3%)
  local copies, waits for them, and re-layouts  11.3 us (2%)
  starting transfers between devices  5.4 us (1%)
    all_gather x2, waiting for transfers between devices, hidden_gather(): return lax.all_gather(row_values, 'row', axis=0, tiled=True)  63.1 us
    reduce_scatter x1, waiting for transfers between devices, on_device(): lax.psum_scatter(plain_product(gathered_two, up_matrix), 'row', scatter_d...  59.9 us
    reduce_scatter x3, waiting for transfers between devices, row_reduce(): lax.psum_scatter(row_partial_term(), 'row', scatter_dimension=0, tiled=True)  59 us
    all_gather x4, blocking collectives, token_gather(): return lax.all_gather(row_values, 'col', axis=0, tiled=True)  58.3 us
    psum x4, blocking collectives, width_total(): return lax.psum(row_values, 'row')  40.1 us
    reduce_scatter x4, waiting for transfers between devices, col_reduce(): lax.psum_scatter(col_partial_term(), 'col', scatter_dimension=0, tiled=True)  33.7 us
    all_gather x2, blocking collectives, hidden_gather(): return lax.all_gather(row_values, 'row', axis=0, tiled=True)  23.3 us
    psum x1, blocking collectives, on_device(): lax.psum(jnp.stack([gain_one_part, gain_two_part]), ('dp', 'col'))  15.2 us
  transfers between devices with their start and end apart: 17, of which 10 were waited for; matrix products, arithmetic and copies ran while one was open for 10% of the time, Pallas kernels for 0%

commit v1 on v0

v1 whole, which is shorter than its diff:
```python
import itertools
import math

import jax
import jax.numpy as jnp
from jax import lax
from jax.experimental import pallas as pl
from jax.experimental.pallas import tpu as pltpu
from jax.sharding import PartitionSpec as P

D = 1024
KERNEL = 3
STEP = 4


eps_norm = 1e-05
beta_first = 0.9
beta_second = 0.999
eps_adam = 1e-08
matrix_rate = 0.01
small_rate = 0.1
decay_rate = 0.1


def shifted(x, axis, by):
    devices = lax.axis_size(axis)
    pairs = [(i, i + by) for i in range(devices) if 0 <= i + by < devices]
    return lax.ppermute(x, axis, pairs)


def plain_product(left_side, right_side):
    return jnp.dot(left_side, right_side, preferred_element_type=jnp.float32)


def contract_rows(left_side, right_side):
    return lax.dot_general(
        left_side, right_side, (((0,), (0,)), ((), ())), preferred_element_type=jnp.float32
    )


def contract_cols(left_side, right_side):
    return lax.dot_general(
        left_side, right_side, (((1,), (1,)), ((), ())), preferred_element_type=jnp.float32
    )


def adam_step(parameter, gradient, moments, step_rate, decay_weight):
    first_moment = beta_first * moments[0] + (1.0 - beta_first) * gradient
    second_moment = beta_second * moments[1] + (1.0 - beta_second) * gradient * gradient
    first_hat = first_moment / (1.0 - beta_first**STEP)
    second_hat = second_moment / (1.0 - beta_second**STEP)
    update = first_hat / (jnp.sqrt(second_hat) + eps_adam) + decay_weight * parameter
    return (parameter - step_rate * update, jnp.stack([first_moment, second_moment]))


def exchange(ids, axes, gathers=(), swaps=()):
    sizes = [lax.axis_size(axis) for axis in axes]
    devices = math.prod(sizes)
    arrays = tuple(gathers) + tuple(swaps)
    count, whole = len(arrays), len(gathers)
    shapes = [x.shape for x in gathers] + [x.shape[1:] for x in swaps]

    def kernel(*refs):
        sources, targets = refs[:count], refs[count : 2 * count]
        send_sem, recv_sem, own_sem = refs[2 * count :]
        me = jnp.int32(0)
        for axis, size in zip(axes, sizes):
            me = me * size + lax.axis_index(axis)

        def coordinates(index):
            place = {}
            for axis, size in reversed(list(zip(axes, sizes))):
                place[axis] = lax.rem(index, size)
                index = index // size
            return place

        peers = [lax.rem(me + step, devices) for step in range(1, devices)]
        barrier = pltpu.get_barrier_semaphore()
        for peer in peers:
            pl.semaphore_signal(
                barrier,
                inc=1,
                device_id=coordinates(peer),
                device_id_type=pl.DeviceIdType.MESH,
            )
        pl.semaphore_wait(barrier, devices - 1)
        remote, own = [], []
        for item in range(count):
            for step, peer in enumerate(peers):
                copy = pltpu.make_async_remote_copy(
                    src_ref=sources[item] if item < whole else sources[item].at[peer],
                    dst_ref=targets[item].at[me],
                    send_sem=send_sem.at[item, step],
                    recv_sem=recv_sem.at[item, step],
                    device_id=coordinates(peer),
                    device_id_type=pl.DeviceIdType.MESH,
                )
                copy.start()
                remote.append(copy)
        for item in range(count):
            copy = pltpu.make_async_copy(
                sources[item] if item < whole else sources[item].at[me],
                targets[item].at[me],
                own_sem.at[item],
            )
            copy.start()
            own.append(copy)
        for copy in own + remote:
            copy.wait()

    return pl.pallas_call(
        kernel,
        out_shape=[
            jax.ShapeDtypeStruct((devices,) + tuple(shape), x.dtype)
            for shape, x in zip(shapes, arrays)
        ],
        in_specs=[pl.BlockSpec(memory_space=pl.ANY)] * count,
        out_specs=[pl.BlockSpec(memory_space=pltpu.VMEM)] * count,
        scratch_shapes=[
            pltpu.SemaphoreType.DMA((count, devices - 1)),
            pltpu.SemaphoreType.DMA((count, devices - 1)),
            pltpu.SemaphoreType.DMA((count,)),
        ],
        compiler_params=pltpu.CompilerParams(collective_id=next(ids), has_side_effects=True),
    )(*arrays)


def flat_rows(gathered):
    return gathered.reshape((-1,) + gathered.shape[2:])


def row_blocks(partial, axis):
    devices = lax.axis_size(axis)
    return partial.astype(jnp.bfloat16).reshape((devices, -1) + partial.shape[1:])


def added(blocks):
    total = blocks[0].astype(jnp.float32)
    for index in range(1, blocks.shape[0]):
        total = total + blocks[index].astype(jnp.float32)
    return total


def width_total(ids, row_values):
    (parts,) = exchange(ids, ("row",), gathers=[row_values[None, :]])
    return added(parts)[0]


def inverse_rms(ids, residual):
    row_total = width_total(ids, jnp.sum(residual * residual, axis=1))
    return lax.rsqrt(row_total / D + eps_norm)[:, None]


def norm_back(ids, residual, inverse, gain_row, d_normed):
    scaled = d_normed * gain_row
    row_total = width_total(ids, jnp.sum(scaled * residual, axis=1))[:, None] / D
    d_residual = inverse * (scaled - residual * inverse * inverse * row_total)
    gain_part = jnp.sum(d_normed * residual * inverse, axis=0)
    return (d_residual, gain_part)


def on_device(
    block_input,
    out_cot,
    proj_weight,
    conv_weight,
    mixer_weight,
    up_weight,
    down_weight,
    norm_gains,
    proj_moments,
    conv_moments,
    mixer_moments,
    up_moments,
    down_moments,
    gains_moments,
):
    ids = itertools.count()
    low = jnp.bfloat16
    wide_proj, conv_wide, wide_mixer, wide_up, wide_down = exchange(
        ids,
        ("dp",),
        gathers=[
            proj_weight.astype(low).transpose(1, 0, 2),
            conv_weight.astype(low),
            mixer_weight.astype(low),
            up_weight.astype(low).transpose(1, 0, 2),
            down_weight.astype(low),
        ],
    )
    replicas = wide_proj.shape[0]
    width_local = proj_weight.shape[0]
    shard_width = proj_weight.shape[2]
    shard_units = up_weight.shape[2]
    channels = replicas * shard_width
    units = replicas * shard_units
    proj_matrix = wide_proj.transpose(2, 1, 0, 3).reshape(width_local, 3 * channels)
    up_matrix = wide_up.transpose(2, 1, 0, 3).reshape(width_local, 2 * units)
    wide_mixer = flat_rows(wide_mixer)
    wide_down = flat_rows(wide_down)
    conv_taps = conv_wide.transpose(1, 0, 2).reshape(KERNEL, channels).astype(jnp.float32)
    gain_one = norm_gains[0]
    gain_two = norm_gains[1]
    history = KERNEL - 1
    inverse_one = inverse_rms(ids, block_input)
    normed_one = (block_input * inverse_one * gain_one).astype(low)
    gathered_one, gathered_cot = map(
        flat_rows, exchange(ids, ("col",), gathers=[normed_one, out_cot.astype(low)])
    )
    inner_rows = gathered_one.shape[0] // lax.axis_size("row")
    projected, d_hidden = map(
        added,
        exchange(
            ids,
            ("row",),
            swaps=[
                row_blocks(plain_product(gathered_one, proj_matrix), "row"),
                row_blocks(contract_cols(gathered_cot, wide_down), "row"),
            ],
        ),
    )
    gate_b = projected[:, :channels]
    gate_c = projected[:, channels : 2 * channels]
    values_x = projected[:, 2 * channels :]
    mixed_input = gate_b * values_x
    left_rim = shifted(mixed_input[inner_rows - history :], "row", 1)
    padded = jnp.concatenate([left_rim, mixed_input], axis=0)
    convolved = conv_taps[0] * padded[0:inner_rows]
    for offset in range(1, KERNEL):
        convolved = convolved + conv_taps[offset] * padded[offset : offset + inner_rows]
    gated = (gate_c * convolved).astype(low)
    gathered_gated = flat_rows(exchange(ids, ("row",), gathers=[gated])[0])
    mixer_out = added(
        exchange(
            ids,
            ("col",),
            swaps=[row_blocks(plain_product(gathered_gated, wide_mixer), "col")],
        )[0]
    )
    residual_two = block_input + mixer_out
    inverse_two = inverse_rms(ids, residual_two)
    normed_two = (residual_two * inverse_two * gain_two).astype(low)
    gathered_two = flat_rows(exchange(ids, ("col",), gathers=[normed_two])[0])
    gate_up = added(
        exchange(
            ids, ("row",), swaps=[row_blocks(plain_product(gathered_two, up_matrix), "row")]
        )[0]
    )
    gate_pre = gate_up[:, :units]
    lifted = gate_up[:, units:]
    sigmoid_gate = jax.nn.sigmoid(gate_pre)
    swish_gate = gate_pre * sigmoid_gate
    hidden = (swish_gate * lifted).astype(low)
    d_gate = d_hidden * lifted * sigmoid_gate * (1.0 + gate_pre * (1.0 - sigmoid_gate))
    d_lifted = d_hidden * swish_gate
    d_gate_up = jnp.concatenate([d_gate, d_lifted], axis=1).astype(low)
    gathered_hidden, gathered_dgate = map(
        flat_rows, exchange(ids, ("row",), gathers=[hidden, d_gate_up])
    )
    ffn_out, d_normed_two = map(
        added,
        exchange(
            ids,
            ("col",),
            swaps=[
                row_blocks(plain_product(gathered_hidden, wide_down), "col"),
                row_blocks(contract_cols(gathered_dgate, up_matrix), "col"),
            ],
        ),
    )
    block_output = residual_two + ffn_out
    down_part = contract_rows(gathered_hidden, gathered_cot)
    up_part = contract_rows(gathered_two, gathered_dgate)
    d_norm_two, gain_two_part = norm_back(ids, residual_two, inverse_two, gain_two, d_normed_two)
    d_residual = out_cot + d_norm_two
    gathered_dres = flat_rows(exchange(ids, ("col",), gathers=[d_residual.astype(low)])[0])
    d_gated = added(
        exchange(
            ids,
            ("row",),
            swaps=[row_blocks(contract_cols(gathered_dres, wide_mixer), "row")],
        )[0]
    )
    mixer_part = contract_rows(gathered_gated, gathered_dres)
    d_convolved = d_gated * gate_c
    d_gate_c = d_gated * convolved
    next_rim = shifted(d_convolved[:history], "row", -1)
    extended = jnp.concatenate([d_convolved, next_rim], axis=0)
    d_mixed = conv_taps[history] * extended[0:inner_rows]
    for offset in range(1, KERNEL):
        d_mixed = d_mixed + conv_taps[history - offset] * extended[offset : offset + inner_rows]
    conv_part = jnp.stack(
        [
            jnp.sum(d_convolved * padded[offset : offset + inner_rows], axis=0)
            for offset in range(KERNEL)
        ]
    )
    d_projected = jnp.concatenate([d_mixed * values_x, d_gate_c, d_mixed * gate_b], axis=1).astype(
        low
    )
    gathered_dproj = flat_rows(exchange(ids, ("row",), gathers=[d_projected])[0])
    proj_part = contract_rows(gathered_one, gathered_dproj)
    d_normed_one = added(
        exchange(
            ids,
            ("col",),
            swaps=[row_blocks(contract_cols(gathered_dproj, proj_matrix), "col")],
        )[0]
    )
    d_norm_one, gain_one_part = norm_back(ids, block_input, inverse_one, gain_one, d_normed_one)
    input_grad = d_residual + d_norm_one
    proj_grad, mixer_grad, up_grad, down_grad = map(
        added,
        exchange(
            ids,
            ("dp",),
            swaps=[
                proj_part.astype(low)
                .reshape(width_local, 3, replicas, shard_width)
                .transpose(2, 1, 0, 3),
                row_blocks(mixer_part, "dp"),
                up_part.astype(low)
                .reshape(width_local, 2, replicas, shard_units)
                .transpose(2, 1, 0, 3),
                row_blocks(down_part, "dp"),
            ],
        ),
    )
    proj_grad = proj_grad.transpose(1, 0, 2)
    up_grad = up_grad.transpose(1, 0, 2)
    conv_total = added(exchange(ids, ("dp", "row"), gathers=[conv_part])[0])
    conv_grad = lax.dynamic_slice_in_dim(
        conv_total, lax.axis_index("dp") * shard_width, shard_width, 1
    )
    gains_part = jnp.stack([gain_one_part, gain_two_part])
    gains_grad = added(exchange(ids, ("dp", "col"), gathers=[gains_part])[0])
    proj_new, proj_moments_new = adam_step(
        proj_weight, proj_grad, proj_moments, matrix_rate, decay_rate
    )
    conv_new, conv_moments_new = adam_step(conv_weight, conv_grad, conv_moments, small_rate, 0.0)
    mixer_new, mixer_moments_new = adam_step(
        mixer_weight, mixer_grad, mixer_moments, matrix_rate, decay_rate
    )
    up_new, up_moments_new = adam_step(up_weight, up_grad, up_moments, matrix_rate, decay_rate)
    down_new, down_moments_new = adam_step(
        down_weight, down_grad, down_moments, matrix_rate, decay_rate
    )
    gains_new, gains_moments_new = adam_step(norm_gains, gains_grad, gains_moments, small_rate, 0.0)
    return (
        block_output,
        input_grad,
        proj_grad,
        conv_grad,
        mixer_grad,
        up_grad,
        down_grad,
        gains_grad,
        proj_new,
        conv_new,
        mixer_new,
        up_new,
        down_new,
        gains_new,
        proj_moments_new,
        conv_moments_new,
        mixer_moments_new,
        up_moments_new,
        down_moments_new,
        gains_moments_new,
    )


def solution(mesh):
    in_specs = (
        P(("dp", "col"), "row"),
        P(("dp", "col"), "row"),
        P("row", None, ("dp", "col")),
        P(None, ("dp", "col")),
        P(("dp", "col"), "row"),
        P("row", None, ("dp", "col")),
        P(("dp", "col"), "row"),
        P(None, "row"),
        P(None, "row", None, ("dp", "col")),
        P(None, None, ("dp", "col")),
        P(None, ("dp", "col"), "row"),
        P(None, "row", None, ("dp", "col")),
        P(None, ("dp", "col"), "row"),
        P(None, None, "row"),
    )
    out_specs = (
        P(("dp", "col"), "row"),
        P(("dp", "col"), "row"),
        P("row", None, ("dp", "col")),
        P(None, ("dp", "col")),
        P(("dp", "col"), "row"),
        P("row", None, ("dp", "col")),
        P(("dp", "col"), "row"),
        P(None, "row"),
        P("row", None, ("dp", "col")),
        P(None, ("dp", "col")),
        P(("dp", "col"), "row"),
        P("row", None, ("dp", "col")),
        P(("dp", "col"), "row"),
        P(None, "row"),
        P(None, "row", None, ("dp", "col")),
        P(None, None, ("dp", "col")),
        P(None, ("dp", "col"), "row"),
        P(None, "row", None, ("dp", "col")),
        P(None, ("dp", "col"), "row"),
        P(None, None, "row"),
    )
    return jax.shard_map(
        on_device, mesh=mesh, in_specs=in_specs, out_specs=out_specs, check_vma=False
    )
```

time: 476 us -> 346 us (0.73)
  Pallas kernels: 0 us -> 231 us
  waiting for transfers between devices: 220 us -> 0.01 us
  blocking collectives: 159 us -> 0 us
  local copies, waits for them, and re-layouts: 11.3 us -> 30.6 us
  other arithmetic: 35.6 us -> 51.2 us
  between operations: 15.8 us -> 1.21 us
    pallas_call x0 -> x20, Pallas kernels: none -> 231 us  [exchange(): pl.pallas_call(kernel, out_shape=[jax.ShapeDtypeStruct((devices,) + tuple...]
    reduce_scatter x12 -> x0, waiting for transfers between devices: 153 us -> none  [the longest x1 59.9 us: on_device(): lax.psum_scatter(plain_product(gathered_two, up_matrix), 'row', scatter_d...]
    all_gather x10 -> x0, blocking collectives: 89.6 us -> none  [the longest x4 58.3 us: token_gather(): return lax.all_gather(row_values, 'col', axis=0, tiled=True)]
    psum x6 -> x0, blocking collectives: 69 us -> none  [the longest x4 40.1 us: width_total(): return lax.psum(row_values, 'row')]
    all_gather x3 -> x0, waiting for transfers between devices: 63.1 us -> none  [the longest x2 63.1 us: hidden_gather(): return lax.all_gather(row_values, 'row', axis=0, tiled=True)]
    add x1 -> x7, other arithmetic: 1.67 us -> 7.34 us  [the longest x3 4 us: added(): total = total + blocks[index].astype(jnp.float32)]
    convert_element_type x10, other arithmetic: 5.58 us -> 11 us  [the longest x1 1.99 us: on_device(): d_residual.astype(low)]
    another operation x13 -> x11, other arithmetic: 14.9 us -> 10.3 us  [adam_step(): jnp.stack([first_moment, second_moment])]
  transfers between devices with their start and end apart: 17 -> 2, of which waited for: 10 -> 0; matrix products, arithmetic and copies ran while one was open for 10% -> 6% of each run, Pallas kernels for 0% -> 2%
where the time goes in v1:
time: 346 us; the launch traced here: 344 us
  Pallas kernels  231 us (67%)
  other arithmetic  51.2 us (15%)
  local copies, waits for them, and re-layouts  30.6 us (9%)
  matrix products  24.4 us (7%)
  starting transfers between devices  5.38 us (2%)
    pallas_call x20, Pallas kernels, exchange(): pl.pallas_call(kernel, out_shape=[jax.ShapeDtypeStruct((devices,) + tuple...  231 us
    unnamed x101, local copies, waits for them, and re-layouts  12.7 us
    another operation x11, other arithmetic, adam_step(): jnp.stack([first_moment, second_moment])  10.3 us
    dot_general x4, matrix products, contract_rows(): lax.dot_general(left_side, right_side, (((0,), (0,)), ((), ())), preferre...  9.35 us
    dot_general x4, matrix products, plain_product(): return jnp.dot(left_side, right_side, preferred_element_type=jnp.float32)  8 us
    dot_general x4, matrix products, contract_cols(): lax.dot_general(left_side, right_side, (((1,), (1,)), ((), ())), preferre...  7.05 us
  transfers between devices with their start and end apart: 2, of which 0 were waited for; matrix products, arithmetic and copies ran while one was open for 6% of the time, Pallas kernels for 2%

profile of v1, /device:TPU:0, one launch (start us, length us, event | category | flops | bytes accessed | tf_op | source)
XLA Modules:
  0.0 344.1 jit_solution(14084468114262536188)
XLA Ops:
  1.4 1.5 multiply_reduce_fusion.6
  2.9 6.9 %shard_map.293 = f32[4,1,128]{2,1,0:T(1,128)} custom-call(f32[1,128]{1,0:T(1,128)} %bitcast.313), custom_call_target="tpu_custom_call" | custom-call | tf_op jit(solution)/shard_map/pallas_call | solution.py:111
  10.5 1.5 convert_element_type.247.refs_1_
  12.1 1.4 convert_element_type.251
  17.2 4.7 %shard_map.295 = (bf16[2,3,256,128]{3,2,1,0:T(8,128)(2,1)}, bf16[2,3,128]{2,1,0:T(4,128)(2,1)}, bf16[2,128,256]{2,1,0:T(8,128)(2,1)}, bf16[2,2,256,576]{3,2,1,0:T(8,128)(2,1)}, bf16[2,576,256]{2,1,0:T(8,128)(2,1)}) custom-call(bf16[3,256,128]{2,1,0:T(8,128)(2,1)} %convert_bitcast_fusion.refs_0_, bf16[3,128]{1,0:T(4,128)(2,1)} %convert_element_type.249.refs_1_, ...), custom_call_target="tpu_custom_call" | custom-call | tf_op jit(solution)/shard_map/pallas_call | solution.py:111
  21.9 1.2 copy.71
  23.9 15.8 %shard_map.294 = (bf16[4,128,256]{2,1,0:T(8,128)(2,1)}, bf16[4,128,256]{2,1,0:T(8,128)(2,1)}) custom-call(bf16[128,256]{1,0:T(8,128)(2,1)} %multiply_convert_fusion.5.refs_0_, bf16[128,256]{1,0:T(8,128)(2,1)} %convert_element_type.247.refs_1_), custom_call_target="tpu_custom_call" | custom-call | tf_op jit(solution)/shard_map/pallas_call | solution.py:111
  39.7 2.5 convolution_convert_fusion.1
  42.3 1.3 convolution_convert_fusion.2
  43.6 26.2 %shard_map.296 = (bf16[4,128,768]{2,1,0:T(8,128)(2,1)}, bf16[4,128,1152]{2,1,0:T(8,128)(2,1)}) custom-call(bf16[4,128,768]{2,1,0:T(8,128)(2,1)} %bitcast.269, bf16[4,128,1152]{2,1,0:T(8,128)(2,1)} %bitcast.264), custom_call_target="tpu_custom_call" | custom-call | tf_op jit(solution)/shard_map/pallas_call | solution.py:111
  69.8 1.3 add_bitcast_fusion.3
  71.8 3.9 %collective-permute-start = (f32[2,256]{1,0:T(2,128)}, f32[2,256]{1,0:T(2,128)}, u32[]{:S(2)}, u32[]{:S(2)}) collective-permute-start(f32[2,256]{1,0:T(2,128)} %slice.412), channel_id=1, source_target_pairs={{0,4},{4,8},{8,12},{1,5},{5,9},{9,13},{2,6},{6,10},{10,14},{3,7},{... | collective-permute-start | bytes 6152 | tf_op jit(solution)/shard_map/ppermute | solution.py:28
  76.3 3.3 fusion.62
  80.5 2.4 copy.72
  82.9 1.7 copy.97
  84.6 2.8 copy.98
  87.4 1.8 multiply_convert_fusion.4
  89.2 6.4 %shard_map.297 = bf16[4,128,256]{2,1,0:T(8,128)(2,1)} custom-call(bf16[128,256]{1,0:T(8,128)(2,1)} %get-tuple-element.138.refs_0_), custom_call_target="tpu_custom_call" | custom-call | tf_op jit(solution)/shard_map/pallas_call | solution.py:111
  95.6 1.9 convolution_convert_fusion.7
  97.5 8.7 %shard_map.298 = bf16[4,128,256]{2,1,0:T(8,128)(2,1)} custom-call(bf16[4,128,256]{2,1,0:T(8,128)(2,1)} %bitcast.279), custom_call_target="tpu_custom_call" | custom-call | tf_op jit(solution)/shard_map/pallas_call | solution.py:111
  106.2 2.1 multiply_reduce_fusion.5
  108.4 5.3 %shard_map.299 = f32[4,1,128]{2,1,0:T(1,128)} custom-call(f32[1,128]{1,0:T(1,128)} %bitcast.311), custom_call_target="tpu_custom_call" | custom-call | tf_op jit(solution)/shard_map/pallas_call | solution.py:111
  114.9 1.6 multiply_convert_fusion.3.refs_0_
  116.5 8.5 %shard_map.300 = bf16[4,128,256]{2,1,0:T(8,128)(2,1)} custom-call(bf16[128,256]{1,0:T(8,128)(2,1)} %multiply_convert_fusion.3.refs_0_), custom_call_target="tpu_custom_call" | custom-call | tf_op jit(solution)/shard_map/pallas_call | solution.py:111
  124.9 3.6 %convolution_convert_fusion = bf16[512,2304]{1,0:T(8,128)(2,1)} fusion(bf16[512,256]{1,0:T(8,128)(2,1)} %bitcast.274, bf16[256,2304]{0,1:T(8,128)(2,1)} %bitcast.265), kind=kOutput, calls=%fused_computation | convolution fusion | flops 605159424 | bytes 3801088 | tf_op jit(solution)/shard_map/dot_general | solution.py:32
  128.5 25.1 %shard_map.301 = bf16[4,128,2304]{2,1,0:T(8,128)(2,1)} custom-call(bf16[4,128,2304]{2,1,0:T(8,128)(2,1)} %bitcast.260), custom_call_target="tpu_custom_call" | custom-call | tf_op jit(solution)/shard_map/pallas_call | solution.py:111
  153.6 2.0 add_bitcast_fusion.1
  157.6 42.1 %shard_map.302 = (bf16[4,128,1152]{2,1,0:T(8,128)(2,1)}, bf16[4,128,2304]{2,1,0:T(8,128)(2,1)}) custom-call(bf16[128,1152]{1,0:T(8,128)(2,1)} %get-tuple-element.151.refs_0_, bf16[128,2304]{1,0:T(8,128)(2,1)} %pad_maximum_fusion.3.refs_1_), custom_call_target="tpu_custom_call" | custom-call | tf_op jit(solution)/shard_map/pallas_call | solution.py:111
  199.8 3.7 %fusion = bf16[256,2304]{1,0:T(8,128)(2,1)} fusion(bf16[4,128,256]{2,1,0:T(8,128)(2,1)} %shard_map.300, bf16[4,128,2304]{2,1,0:T(8,128)(2,1)} %get-tuple-element.47), kind=kOutput, calls=%fused_computation.2 | convolution fusion | flops 604569600 | bytes 3801088 | tf_op jit(solution)/shard_map/dot_general | solution.py:36
  203.5 1.5 convolution_convert_fusion.5
  205.0 1.3 fusion.1
  206.3 1.2 convolution_convert_fusion.6
  207.5 15.1 %shard_map.303 = (bf16[4,128,256]{2,1,0:T(8,128)(2,1)}, bf16[4,128,256]{2,1,0:T(8,128)(2,1)}) custom-call(bf16[4,128,256]{2,1,0:T(8,128)(2,1)} %bitcast.290, bf16[4,128,256]{2,1,0:T(8,128)(2,1)} %bitcast.289), custom_call_target="tpu_custom_call" | custom-call | tf_op jit(solution)/shard_map/pallas_call | solution.py:111
  222.6 1.7 fusion.40
  224.3 5.3 %shard_map.304 = f32[4,1,128]{2,1,0:T(1,128)} custom-call(f32[1,128]{1,0:T(1,128)} %bitcast.312), custom_call_target="tpu_custom_call" | custom-call | tf_op jit(solution)/shard_map/pallas_call | solution.py:111
  230.3 2.0 fusion.61
  232.3 8.5 %shard_map.305 = bf16[4,128,256]{2,1,0:T(8,128)(2,1)} custom-call(bf16[128,256]{1,0:T(8,128)(2,1)} %get-tuple-element.134.refs_0_), custom_call_target="tpu_custom_call" | custom-call | tf_op jit(solution)/shard_map/pallas_call | solution.py:111
  240.8 2.0 fusion.4
  242.7 1.9 convolution_convert_fusion.4
  244.7 6.8 %shard_map.306 = bf16[4,128,256]{2,1,0:T(8,128)(2,1)} custom-call(bf16[4,128,256]{2,1,0:T(8,128)(2,1)} %bitcast.278), custom_call_target="tpu_custom_call" | custom-call | tf_op jit(solution)/shard_map/pallas_call | solution.py:111
  251.5 1.9 multiply_reduce_fusion.2
  254.6 1.5 collective-permute-start.1
  256.7 6.9 %shard_map.311 = f32[8,3,256]{2,1,0:T(4,128)} custom-call(f32[3,256]{1,0:T(4,128)} %pad_maximum_fusion.8.refs_0_), custom_call_target="tpu_custom_call" | custom-call | tf_op jit(solution)/shard_map/pallas_call | solution.py:111
  264.4 1.3 fusion.56
  265.7 2.4 copy.78
  268.0 2.4 copy.79
  272.2 1.6 pad_maximum_fusion.5.refs_0_
  273.8 13.1 %shard_map.307 = bf16[4,128,768]{2,1,0:T(8,128)(2,1)} custom-call(bf16[128,768]{1,0:T(8,128)(2,1)} %pad_maximum_fusion.5.refs_0_), custom_call_target="tpu_custom_call" | custom-call | tf_op jit(solution)/shard_map/pallas_call | solution.py:111
  286.9 2.3 fusion.3
  290.3 9.2 %shard_map.308 = bf16[4,128,256]{2,1,0:T(8,128)(2,1)} custom-call(bf16[4,128,256]{2,1,0:T(8,128)(2,1)} %bitcast.280), custom_call_target="tpu_custom_call" | custom-call | tf_op jit(solution)/shard_map/pallas_call | solution.py:111
  299.6 1.6 fusion.37
  301.8 7.0 %shard_map.312 = f32[8,2,256]{2,1,0:T(2,128)} custom-call(f32[2,256]{1,0:T(2,128)} %pad_maximum_fusion.11.refs_0_), custom_call_target="tpu_custom_call" | custom-call | tf_op jit(solution)/shard_map/pallas_call | solution.py:111
  310.1 1.2 copy.74
  312.2 4.7 %shard_map.310 = (bf16[2,3,256,128]{3,2,1,0:T(8,128)(2,1)}, bf16[2,128,256]{2,1,0:T(8,128)(2,1)}, bf16[2,2,256,576]{3,2,1,0:T(8,128)(2,1)}, bf16[2,576,256]{2,1,0:T(8,128)(2,1)}) custom-call(bf16[2,3,256,128]{3,2,1,0:T(8,128)(2,1)} %bitcast.275, bf16[2,128,256]{2,1,0:T(8,128)(2,1)} %bitcast.287, bf16[2,2,256,576]{3,2,1,0:T(8,128)(2,1)} %bitcast.262, ...), custom_call_target="tpu_custom_call" | custom-call | tf_op jit(solution)/shard_map/pallas_call | solution.py:111
  317.0 2.6 multiply_add_fusion
  319.6 1.5 multiply_subtract_fusion.1
  321.0 1.2 add_bitcast_fusion
  322.8 2.2 fusion.19
  325.2 2.0 copy.90
  327.2 2.1 fusion.42
  329.3 1.2 fusion.43
  331.0 1.4 copy.88
  332.4 1.4 copy.87
  333.8 5.3 %shard_map.309 = f32[4,1,128]{2,1,0:T(1,128)} custom-call(f32[1,128]{1,0:T(1,128)} %bitcast.310), custom_call_target="tpu_custom_call" | custom-call | tf_op jit(solution)/shard_map/pallas_call | solution.py:111
  (136 shorter events, 26.7 us)
Async XLA Ops:
  10.5 12.7 %copy-start.37 = (f32[128]{0:T(128)}, f32[128]{0:T(128)S(1)}, u32[]{:S(2)}) copy-start(f32[128]{0:T(128)S(1)} %rsqrt_bitcast_fusion.1) | copy-start | bytes 1540
  12.1 2.5 copy-start.9
  13.5 1.9 copy-start.16
  13.5 2.6 copy-start.31
  13.5 3.2 copy-start.42
  15.3 7.9 %copy-start.8 = (f32[128,256]{1,0:T(8,128)S(1)}, f32[128,256]{1,0:T(8,128)}, u32[]{:S(2)}) copy-start(f32[128,256]{1,0:T(8,128)} %param.14) | copy-start | bytes 393220
  21.9 17.8 %copy-start.26 = (bf16[2,576,256]{2,1,0:T(8,128)(2,1)S(1)}, bf16[2,576,256]{2,1,0:T(8,128)(2,1)}, u32[]{:S(2)}) copy-start(bf16[2,576,256]{2,1,0:T(8,128)(2,1)} %get-tuple-element.40) | copy-start | bytes 1769476
  39.7 2.6 copy-start.24
  43.6 32.1 %copy-start.45 = (bf16[2,3,128]{2,1,0:T(4,128)(2,1)S(1)}, bf16[2,3,128]{2,1,0:T(4,128)(2,1)}, u32[]{:S(2)}) copy-start(bf16[2,3,128]{2,1,0:T(4,128)(2,1)} %get-tuple-element.42) | copy-start | bytes 4612
  71.1 8.4 %copy-start.21 = (f32[128,256]{1,0:T(8,128)}, f32[128,256]{1,0:T(8,128)S(1)}, u32[]{:S(2)}) copy-start(f32[128,256]{1,0:T(8,128)S(1)} %slice_multiply_fusion.4) | copy-start | bytes 393220
  71.8 15.6 %collective-permute-start = (f32[2,256]{1,0:T(2,128)}, f32[2,256]{1,0:T(2,128)}, u32[]{:S(2)}, u32[]{:S(2)}) collective-permute-start(f32[2,256]{1,0:T(2,128)} %slice.412), channel_id=1, source_target_pairs={{0,4},{4,8},{8,12},{1,5},{5,9},{9,13},{2,6},{6,10},{10,14},{3,7},{... | collective-permute-start | bytes 6152 | tf_op jit(solution)/shard_map/ppermute | solution.py:28
  76.3 3.3 copy-start.44
  76.3 3.9 %copy-start.5 = (f32[256,2,576]{0,2,1:T(8,128)S(1)}, f32[256,2,576]{0,2,1:T(8,128)}, u32[]{:S(2)}) copy-start(f32[256,2,576]{0,2,1:T(8,128)} %param.19) | copy-start | bytes 3538948
  114.3 0.5 copy-start.39
  153.6 2.0 copy-start.22
  199.7 3.7 %copy-start.7 = (bf16[256,2,2,576]{0,3,2,1:T(8,128)(2,1)S(1)}, bf16[256,2,2,576]{0,3,2,1:T(8,128)(2,1)}, u32[]{:S(2)}) copy-start(bf16[256,2,2,576]{0,3,2,1:T(8,128)(2,1)} %copy.72) | copy-start | bytes 3538948
  199.7 3.7 %copy-start.12 = (bf16[4,128,2304]{2,1,0:T(8,128)(2,1)S(1)}, bf16[4,128,2304]{2,1,0:T(8,128)(2,1)}, u32[]{:S(2)}) copy-start(bf16[4,128,2304]{2,1,0:T(8,128)(2,1)} %get-tuple-element.47) | copy-start | bytes 7077892
  203.5 1.5 copy-start.33
  203.5 1.5 copy-start.46
  205.0 1.3 copy-start.27
  253.4 0.7 copy-start.28
  254.6 16.4 %collective-permute-start.1 = (f32[2,256]{1,0:T(2,128)}, f32[2,256]{1,0:T(2,128)}, u32[]{:S(2)}, u32[]{:S(2)}) collective-permute-start(f32[2,256]{1,0:T(2,128)} %slice.419), channel_id=1, source_target_pairs={{4,0},{8,4},{12,8},{5,1},{9,5},{13,9},{6,2},{10,6},{14,10},{7,3},{... | collective-permute-start | bytes 6152 | tf_op jit(solution)/shard_map/ppermute | solution.py:28
  264.4 1.3 copy-start.41
  268.0 3.0 copy-start.36
  272.2 14.7 %copy-start.25 = (bf16[4,128,256]{2,1,0:T(8,128)(2,1)S(1)}, bf16[4,128,256]{2,1,0:T(8,128)(2,1)}, u32[]{:S(2)}) copy-start(bf16[4,128,256]{2,1,0:T(8,128)(2,1)} %get-tuple-element.37) | copy-start | bytes 786436
  286.9 2.4 copy-start
  289.2 10.3 %copy-start.38 = (f32[128]{0:T(128)S(1)}, f32[128]{0:T(128)}, u32[]{:S(2)}) copy-start(f32[128]{0:T(128)} %copy-done.37) | copy-start | bytes 1540
  289.2 11.9 %copy-start.43 = (f32[256]{0:T(256)S(1)}, f32[256]{0:T(256)}, u32[]{:S(2)}) copy-start(f32[256]{0:T(256)} %get-tuple-element.116) | copy-start | bytes 3076
  289.2 19.5 %copy-start.35 = (f32[2,2,256]{2,1,0:T(2,128)S(1)}, f32[2,2,256]{2,1,0:T(2,128)}, u32[]{:S(2)}) copy-start(f32[2,2,256]{2,1,0:T(2,128)} %param.27) | copy-start | bytes 12292
  289.2 20.3 %copy-start.40 = (f32[2,256]{1,0:T(2,128)S(1)}, f32[2,256]{1,0:T(2,128)}, u32[]{:S(2)}) copy-start(f32[2,256]{1,0:T(2,128)} %param.21) | copy-start | bytes 6148
  309.5 7.4 %copy-start.34 = (f32[1,2,256]{2,1,0:T(2,128)}, f32[1,2,256]{2,1,0:T(2,128)S(1)}, u32[]{:S(2)}) copy-start(f32[1,2,256]{2,1,0:T(2,128)S(1)} %get-tuple-element.122) | copy-start | bytes 6148
  316.9 2.6 copy-start.6
  316.9 2.6 copy-start.10
  317.0 2.6 copy-start.11
  319.5 1.5 copy-start.2
  321.0 1.8 copy-start.1
  327.2 2.1 copy-start.15
  327.2 2.1 copy-start.17
  329.3 1.2 copy-start.18
  329.3 1.7 copy-start.3
  330.4 2.0 copy-start.4
  332.4 8.0 %copy-start.14 = (f32[1,576,256]{2,1,0:T(8,128)S(1)}, f32[1,576,256]{2,1,0:T(8,128)}, u32[]{:S(2)}) copy-start(f32[1,576,256]{2,1,0:T(8,128)} %get-tuple-element.148) | copy-start | bytes 1769476
  333.8 7.7 %copy-start.23 = (f32[2,128,256]{2,1,0:T(8,128)S(1)}, f32[2,128,256]{2,1,0:T(8,128)}, u32[]{:S(2)}) copy-start(f32[2,128,256]{2,1,0:T(8,128)} %param.24) | copy-start | bytes 786436
  333.8 7.7 %copy-start.30 = (bf16[2,128,256]{2,1,0:T(8,128)(2,1)S(1)}, bf16[2,128,256]{2,1,0:T(8,128)(2,1)}, u32[]{:S(2)}) copy-start(bf16[2,128,256]{2,1,0:T(8,128)(2,1)} %get-tuple-element.51) | copy-start | bytes 393220
  340.4 1.9 copy-start.19
  340.4 1.9 copy-start.20
  341.5 1.7 copy-start.13
  341.5 1.7 copy-start.29
  341.5 1.7 copy-start.32

commit v2 on v0

v2 whole, which is shorter than its diff:
```python
import itertools
import math

import jax
import jax.numpy as jnp
from jax import lax
from jax.experimental import pallas as pl
from jax.experimental.pallas import tpu as pltpu
from jax.sharding import PartitionSpec as P

D = 1024
KERNEL = 3
STEP = 4


eps_norm = 1e-05
beta_first = 0.9
beta_second = 0.999
eps_adam = 1e-08
matrix_rate = 0.01
small_rate = 0.1
decay_rate = 0.1


def shifted(x, axis, by):
    devices = lax.axis_size(axis)
    pairs = [(i, i + by) for i in range(devices) if 0 <= i + by < devices]
    return lax.ppermute(x, axis, pairs)


def plain_product(left_side, right_side):
    return jnp.dot(left_side, right_side, preferred_element_type=jnp.float32)


def contract_rows(left_side, right_side):
    return lax.dot_general(
        left_side, right_side, (((0,), (0,)), ((), ())), preferred_element_type=jnp.float32
    )


def contract_cols(left_side, right_side):
    return lax.dot_general(
        left_side, right_side, (((1,), (1,)), ((), ())), preferred_element_type=jnp.float32
    )


def adam_step(parameter, gradient, moments, step_rate, decay_weight):
    first_moment = beta_first * moments[0] + (1.0 - beta_first) * gradient
    second_moment = beta_second * moments[1] + (1.0 - beta_second) * gradient * gradient
    first_hat = first_moment / (1.0 - beta_first**STEP)
    second_hat = second_moment / (1.0 - beta_second**STEP)
    update = first_hat / (jnp.sqrt(second_hat) + eps_adam) + decay_weight * parameter
    is_first = lax.broadcasted_iota(jnp.int32, moments.shape, 0) == 0
    moments_new = jnp.where(
        is_first,
        beta_first * moments + (1.0 - beta_first) * gradient[None],
        beta_second * moments + (1.0 - beta_second) * gradient[None] * gradient[None],
    )
    return (parameter - step_rate * update, moments_new)


def exchange(ids, *items):
    count = len(items)
    groups = []
    for axes, _, _ in items:
        if axes not in groups:
            groups.append(axes)
    sizes = {axes: [lax.axis_size(axis) for axis in axes] for axes in groups}
    devices = {axes: math.prod(sizes[axes]) for axes in groups}
    most = max(devices.values())

    def kernel(*refs):
        sources, targets = refs[:count], refs[count : 2 * count]
        send_sem, recv_sem, own_sem = refs[2 * count :]
        mine, peers = {}, {}
        for axes in groups:
            me = jnp.int32(0)
            for axis, size in zip(axes, sizes[axes]):
                me = me * size + lax.axis_index(axis)
            mine[axes] = me
            peers[axes] = []
            for step in range(1, devices[axes]):
                peer = lax.rem(me + step, devices[axes])
                place, index = {}, peer
                for axis, size in reversed(list(zip(axes, sizes[axes]))):
                    place[axis] = lax.rem(index, size)
                    index = index // size
                peers[axes].append((peer, place))
        barrier = pltpu.get_barrier_semaphore()
        for axes in groups:
            for _, place in peers[axes]:
                pl.semaphore_signal(
                    barrier, inc=1, device_id=place, device_id_type=pl.DeviceIdType.MESH
                )
        pl.semaphore_wait(barrier, sum(len(peers[axes]) for axes in groups))
        copies = []
        for item, (axes, _, whole) in enumerate(items):
            for step, (peer, place) in enumerate(peers[axes]):
                copies.append(
                    pltpu.make_async_remote_copy(
                        src_ref=sources[item] if whole else sources[item].at[peer],
                        dst_ref=targets[item].at[mine[axes]],
                        send_sem=send_sem.at[item, step],
                        recv_sem=recv_sem.at[item, step],
                        device_id=place,
                        device_id_type=pl.DeviceIdType.MESH,
                    )
                )
        for item, (axes, _, whole) in enumerate(items):
            copies.append(
                pltpu.make_async_copy(
                    sources[item] if whole else sources[item].at[mine[axes]],
                    targets[item].at[mine[axes]],
                    own_sem.at[item],
                )
            )
        for copy in copies:
            copy.start()
        for copy in copies:
            copy.wait()

    return pl.pallas_call(
        kernel,
        out_shape=[
            jax.ShapeDtypeStruct(
                (devices[axes],) + tuple(x.shape if whole else x.shape[1:]), x.dtype
            )
            for axes, x, whole in items
        ],
        in_specs=[pl.BlockSpec(memory_space=pl.ANY)] * count,
        out_specs=[pl.BlockSpec(memory_space=pltpu.VMEM)] * count,
        scratch_shapes=[
            pltpu.SemaphoreType.DMA((count, most - 1)),
            pltpu.SemaphoreType.DMA((count, most - 1)),
            pltpu.SemaphoreType.DMA((count,)),
        ],
        compiler_params=pltpu.CompilerParams(collective_id=next(ids), has_side_effects=True),
    )(*[x for _, x, _ in items])


DP, ROW, COL = ("dp",), ("row",), ("col",)


def gather(axes, x):
    return (axes, x, True)


def swap(axes, x):
    blocks = math.prod(lax.axis_size(axis) for axis in axes)
    low = x.astype(jnp.bfloat16)
    return (axes, low.reshape((blocks, -1) + x.shape[1:]), False)


def flat_rows(gathered):
    return gathered.reshape((-1,) + gathered.shape[2:])


def added(blocks):
    total = blocks[0].astype(jnp.float32)
    for index in range(1, blocks.shape[0]):
        total = total + blocks[index].astype(jnp.float32)
    return total


def inverse_rms(row_total):
    return lax.rsqrt(row_total / D + eps_norm)[:, None]


def square_sums(residual):
    return jnp.sum(residual * residual, axis=1)[None, :]


def back_sums(residual, gain_row, d_normed):
    return jnp.sum(d_normed * gain_row * residual, axis=1)[None, :]


def norm_back(residual, inverse, gain_row, d_normed, row_total):
    scaled = d_normed * gain_row
    row_mean = row_total[:, None] / D
    return inverse * (scaled - residual * inverse * inverse * row_mean)


def gain_sums(residual, inverse, d_normed):
    return jnp.sum(d_normed * residual * inverse, axis=0)


def on_device(
    block_input,
    out_cot,
    proj_weight,
    conv_weight,
    mixer_weight,
    up_weight,
    down_weight,
    norm_gains,
    proj_moments,
    conv_moments,
    mixer_moments,
    up_moments,
    down_moments,
    gains_moments,
):
    ids = itertools.count()
    low = jnp.bfloat16
    up_turned = up_weight.transpose(1, 2, 0)
    up_low = up_turned.astype(low)
    stats, wide_proj, conv_wide, wide_mixer, wide_gate, wide_lift, wide_down = exchange(
        ids,
        gather(ROW, square_sums(block_input)),
        gather(DP, proj_weight.astype(low).transpose(1, 0, 2)),
        gather(DP, conv_weight.astype(low)),
        gather(DP, mixer_weight.astype(low)),
        gather(DP, up_low[0]),
        gather(DP, up_low[1]),
        gather(DP, down_weight.astype(low)),
    )
    replicas = wide_proj.shape[0]
    width_local = proj_weight.shape[0]
    shard_width = proj_weight.shape[2]
    channels = replicas * shard_width
    proj_matrix = wide_proj.transpose(2, 1, 0, 3).reshape(width_local, 3 * channels)
    wide_mixer, wide_gate, wide_lift, wide_down = map(
        flat_rows, (wide_mixer, wide_gate, wide_lift, wide_down)
    )
    conv_taps = conv_wide.transpose(1, 0, 2).reshape(KERNEL, channels).astype(jnp.float32)
    gain_one = norm_gains[0]
    gain_two = norm_gains[1]
    history = KERNEL - 1
    inverse_one = inverse_rms(added(stats)[0])
    normed_one = (block_input * inverse_one * gain_one).astype(low)
    gathered_one = flat_rows(exchange(ids, gather(COL, normed_one))[0])
    projected, gathered_cot = exchange(
        ids,
        swap(ROW, plain_product(gathered_one, proj_matrix)),
        gather(COL, out_cot.astype(low)),
    )
    projected = added(projected)
    gathered_cot = flat_rows(gathered_cot)
    inner_rows = projected.shape[0]
    half = wide_down.shape[0] // 256 * 128 or wide_down.shape[0] // 2
    gate_b = projected[:, :channels]
    gate_c = projected[:, channels : 2 * channels]
    values_x = projected[:, 2 * channels :]
    mixed_input = gate_b * values_x
    left_rim = shifted(mixed_input[inner_rows - history :], "row", 1)
    padded = jnp.concatenate([left_rim, mixed_input], axis=0)
    convolved = conv_taps[0] * padded[0:inner_rows]
    for offset in range(1, KERNEL):
        convolved = convolved + conv_taps[offset] * padded[offset : offset + inner_rows]
    gated = (gate_c * convolved).astype(low)
    gathered_gated = flat_rows(exchange(ids, gather(ROW, gated))[0])
    mixer_out, d_hidden_a = exchange(
        ids,
        swap(COL, plain_product(gathered_gated, wide_mixer)),
        swap(ROW, contract_cols(gathered_cot, wide_down[:half])),
    )
    residual_two = block_input + added(mixer_out)
    (stats,) = exchange(ids, gather(ROW, square_sums(residual_two)))
    inverse_two = inverse_rms(added(stats)[0])
    normed_two = (residual_two * inverse_two * gain_two).astype(low)
    gathered_two, d_hidden_b = exchange(
        ids,
        gather(COL, normed_two),
        swap(ROW, contract_cols(gathered_cot, wide_down[half:])),
    )
    gathered_two = flat_rows(gathered_two)
    d_hidden = jnp.concatenate([added(d_hidden_a), added(d_hidden_b)], axis=1)
    gate_pre, lifted = map(
        added,
        exchange(
            ids,
            swap(ROW, contract_cols(gathered_two, wide_gate)),
            swap(ROW, contract_cols(gathered_two, wide_lift)),
        ),
    )
    sigmoid_gate = jax.nn.sigmoid(gate_pre)
    swish_gate = gate_pre * sigmoid_gate
    hidden = (swish_gate * lifted).astype(low)
    d_gate = d_hidden * lifted * sigmoid_gate * (1.0 + gate_pre * (1.0 - sigmoid_gate))
    d_lifted = d_hidden * swish_gate
    gathered_dgate, gathered_dlift = map(
        flat_rows,
        exchange(ids, gather(ROW, d_gate.astype(low)), gather(ROW, d_lifted.astype(low))),
    )
    hidden_half = inner_rows // 2
    d_normed_two, hidden_a = exchange(
        ids,
        swap(
            COL,
            plain_product(gathered_dgate, wide_gate) + plain_product(gathered_dlift, wide_lift),
        ),
        gather(ROW, hidden[:hidden_half]),
    )
    d_normed_two = added(d_normed_two)
    (stats,) = exchange(ids, gather(ROW, back_sums(residual_two, gain_two, d_normed_two)))
    d_residual = out_cot + norm_back(
        residual_two, inverse_two, gain_two, d_normed_two, added(stats)[0]
    )
    gathered_dres, hidden_b = exchange(
        ids, gather(COL, d_residual.astype(low)), gather(ROW, hidden[hidden_half:])
    )
    gathered_dres = flat_rows(gathered_dres)
    gathered_hidden = flat_rows(jnp.concatenate([hidden_a, hidden_b], axis=1))
    (d_gated,) = exchange(ids, swap(ROW, contract_cols(gathered_dres, wide_mixer)))
    d_gated = added(d_gated)
    d_convolved = d_gated * gate_c
    d_gate_c = d_gated * convolved
    next_rim = shifted(d_convolved[:history], "row", -1)
    extended = jnp.concatenate([d_convolved, next_rim], axis=0)
    d_mixed = conv_taps[history] * extended[0:inner_rows]
    for offset in range(1, KERNEL):
        d_mixed = d_mixed + conv_taps[history - offset] * extended[offset : offset + inner_rows]
    conv_part = jnp.stack(
        [
            jnp.sum(d_convolved * padded[offset : offset + inner_rows], axis=0)
            for offset in range(KERNEL)
        ]
    )
    d_projected = jnp.concatenate([d_mixed * values_x, d_gate_c, d_mixed * gate_b], axis=1).astype(
        low
    )
    gathered_dproj, ffn_out, conv_parts = exchange(
        ids,
        gather(ROW, d_projected),
        swap(COL, plain_product(gathered_hidden, wide_down)),
        gather(("dp", "row"), conv_part),
    )
    gathered_dproj = flat_rows(gathered_dproj)
    block_output = residual_two + added(ffn_out)
    proj_part = contract_rows(gathered_one, gathered_dproj).astype(low)
    proj_part = proj_part.reshape(width_local, 3, replicas, shard_width).transpose(2, 1, 0, 3)
    d_normed_one, proj_grad, mixer_grad, up_grad_gate, up_grad_lift, down_grad = map(
        added,
        exchange(
            ids,
            swap(COL, contract_cols(gathered_dproj, proj_matrix)),
            (DP, proj_part, False),
            swap(DP, contract_rows(gathered_gated, gathered_dres)),
            swap(DP, contract_rows(gathered_dgate, gathered_two)),
            swap(DP, contract_rows(gathered_dlift, gathered_two)),
            swap(DP, contract_rows(gathered_hidden, gathered_cot)),
        ),
    )
    gains_part = jnp.stack(
        [
            gain_sums(block_input, inverse_one, d_normed_one),
            gain_sums(residual_two, inverse_two, d_normed_two),
        ]
    )
    stats, gains_parts = exchange(
        ids,
        gather(ROW, back_sums(block_input, gain_one, d_normed_one)),
        gather(("dp", "col"), gains_part),
    )
    input_grad = d_residual + norm_back(
        block_input, inverse_one, gain_one, d_normed_one, added(stats)[0]
    )
    proj_grad = proj_grad.transpose(1, 0, 2)
    up_grad = jnp.stack([up_grad_gate, up_grad_lift]).transpose(2, 0, 1)
    conv_grad = lax.dynamic_slice_in_dim(
        added(conv_parts), lax.axis_index("dp") * shard_width, shard_width, 1
    )
    gains_grad = added(gains_parts)
    proj_new, proj_moments_new = adam_step(
        proj_weight, proj_grad, proj_moments, matrix_rate, decay_rate
    )
    conv_new, conv_moments_new = adam_step(conv_weight, conv_grad, conv_moments, small_rate, 0.0)
    mixer_new, mixer_moments_new = adam_step(
        mixer_weight, mixer_grad, mixer_moments, matrix_rate, decay_rate
    )
    up_new, up_moments_new = adam_step(up_weight, up_grad, up_moments, matrix_rate, decay_rate)
    down_new, down_moments_new = adam_step(
        down_weight, down_grad, down_moments, matrix_rate, decay_rate
    )
    gains_new, gains_moments_new = adam_step(norm_gains, gains_grad, gains_moments, small_rate, 0.0)
    return (
        block_output,
        input_grad,
        proj_grad,
        conv_grad,
        mixer_grad,
        up_grad,
        down_grad,
        gains_grad,
        proj_new,
        conv_new,
        mixer_new,
        up_new,
        down_new,
        gains_new,
        proj_moments_new,
        conv_moments_new,
        mixer_moments_new,
        up_moments_new,
        down_moments_new,
        gains_moments_new,
    )


def solution(mesh):
    in_specs = (
        P(("dp", "col"), "row"),
        P(("dp", "col"), "row"),
        P("row", None, ("dp", "col")),
        P(None, ("dp", "col")),
        P(("dp", "col"), "row"),
        P("row", None, ("dp", "col")),
        P(("dp", "col"), "row"),
        P(None, "row"),
        P(None, "row", None, ("dp", "col")),
        P(None, None, ("dp", "col")),
        P(None, ("dp", "col"), "row"),
        P(None, "row", None, ("dp", "col")),
        P(None, ("dp", "col"), "row"),
        P(None, None, "row"),
    )
    out_specs = (
        P(("dp", "col"), "row"),
        P(("dp", "col"), "row"),
        P("row", None, ("dp", "col")),
        P(None, ("dp", "col")),
        P(("dp", "col"), "row"),
        P("row", None, ("dp", "col")),
        P(("dp", "col"), "row"),
        P(None, "row"),
        P("row", None, ("dp", "col")),
        P(None, ("dp", "col")),
        P(("dp", "col"), "row"),
        P("row", None, ("dp", "col")),
        P(("dp", "col"), "row"),
        P(None, "row"),
        P(None, "row", None, ("dp", "col")),
        P(None, None, ("dp", "col")),
        P(None, ("dp", "col"), "row"),
        P(None, "row", None, ("dp", "col")),
        P(None, ("dp", "col"), "row"),
        P(None, None, "row"),
    )
    return jax.shard_map(
        on_device, mesh=mesh, in_specs=in_specs, out_specs=out_specs, check_vma=False
    )
```

time: 476 us -> 267 us (0.56)
  waiting for transfers between devices: 220 us -> 3.4 us
  Pallas kernels: 0 us -> 180 us
  blocking collectives: 159 us -> 0 us
  between operations: 15.8 us -> 1.34 us
    pallas_call x0 -> x16, Pallas kernels: none -> 180 us  [exchange(): pl.pallas_call(kernel, out_shape=[jax.ShapeDtypeStruct((devices[axes],) +...]
    reduce_scatter x12 -> x0, waiting for transfers between devices: 153 us -> none  [the longest x1 59.9 us: on_device(): lax.psum_scatter(plain_product(gathered_two, up_matrix), 'row', scatter_d...]
    all_gather x10 -> x0, blocking collectives: 89.6 us -> none  [the longest x4 58.3 us: token_gather(): return lax.all_gather(row_values, 'col', axis=0, tiled=True)]
    psum x6 -> x0, blocking collectives: 69 us -> none  [the longest x4 40.1 us: width_total(): return lax.psum(row_values, 'row')]
    all_gather x3 -> x0, waiting for transfers between devices: 63.1 us -> none  [the longest x2 63.1 us: hidden_gather(): return lax.all_gather(row_values, 'row', axis=0, tiled=True)]
    another operation x17 -> x3, other arithmetic: 18.2 us -> 0.66 us  [the longest x1 0.58 us: on_device(): jnp.stack([gain_sums(block_input, inverse_one, d_normed_one), gain_sums(r...]
    select_n x0 -> x6, other arithmetic: none -> 6.24 us  [adam_step(): jnp.where(is_first, beta_first * moments + (1.0 - beta_first) * gradient[...]
    convert_element_type x10 -> x12, other arithmetic: 5.58 us -> 11.8 us  [the longest x1 2.58 us: on_device(): hidden = (swish_gate * lifted).astype(low)]
  transfers between devices with their start and end apart: 17 -> 2, of which waited for: 10 -> 1; matrix products, arithmetic and copies ran while one was open for 10% -> 1% of each run, Pallas kernels for 0% -> 0%
where the time goes in v2:
time: 267 us
  Pallas kernels  180 us (67%)
  other arithmetic  38.9 us (15%)
  matrix products  26.2 us (10%)
  local copies, waits for them, and re-layouts  11.9 us (4%)
  starting transfers between devices  4.84 us (2%)
  waiting for transfers between devices  3.4 us (1%)
    pallas_call x16, Pallas kernels, exchange(): pl.pallas_call(kernel, out_shape=[jax.ShapeDtypeStruct((devices[axes],) +...  180 us
    dot_general x5, matrix products, contract_rows(): lax.dot_general(left_side, right_side, (((0,), (0,)), ((), ())), preferre...  9.29 us
    dot_general x6, matrix products, contract_cols(): lax.dot_general(left_side, right_side, (((1,), (1,)), ((), ())), preferre...  8.56 us
    dot_general x5, matrix products, plain_product(): return jnp.dot(left_side, right_side, preferred_element_type=jnp.float32)  8.35 us
    select_n x6, other arithmetic, adam_step(): jnp.where(is_first, beta_first * moments + (1.0 - beta_first) * gradient[...  6.24 us
    unnamed x107, local copies, waits for them, and re-layouts  6.07 us
  transfers between devices with their start and end apart: 2, of which 1 were waited for; matrix products, arithmetic and copies ran while one was open for 1% of the time, Pallas kernels for 0%

profile of v2, /device:TPU:0, one launch (start us, length us, event | category | flops | bytes accessed | tf_op | source)
XLA Modules:
  0.0 266.6 jit_solution(7675808316084198853)
XLA Ops:
  0.7 1.4 convert_bitcast_fusion
  2.1 0.8 slice_bitcast_fusion
  3.0 0.7 convert_element_type.308.refs_6_
  3.7 0.7 convert_bitcast_fusion.1.refs_1_
  6.3 8.4 %shard_map.293 = (f32[4,1,128]{2,1,0:T(1,128)}, bf16[2,3,256,128]{3,2,1,0:T(8,128)(2,1)}, bf16[2,3,128]{2,1,0:T(4,128)(2,1)}, bf16[2,128,256]{2,1,0:T(8,128)(2,1...) custom-call(f32[1,128]{1,0:T(1,128)} %bitcast.380, ...), custom_call_target="tpu_custom_call" | custom-call | tf_op jit(solution)/shard_map/pallas_call | solution.py:122
  15.4 0.7 multiply_convert_fusion.5.refs_0_
  16.1 10.3 %shard_map.294 = bf16[4,128,256]{2,1,0:T(8,128)(2,1)} custom-call(bf16[128,256]{1,0:T(8,128)(2,1)} %multiply_convert_fusion.5.refs_0_), custom_call_target="tpu_custom_call" | custom-call | tf_op jit(solution)/shard_map/pallas_call | solution.py:122
  26.4 1.2 copy.41
  28.2 2.2 convolution_convert_fusion.2
  30.4 12.9 %shard_map.295 = (bf16[4,128,768]{2,1,0:T(8,128)(2,1)}, bf16[4,128,256]{2,1,0:T(8,128)(2,1)}) custom-call(bf16[4,128,768]{2,1,0:T(8,128)(2,1)} %bitcast.328, bf16[128,256]{1,0:T(8,128)(2,1)} %convert_element_type.311.refs_1_), custom_call_target="tpu_custom_call" | custom-call | tf_op jit(solution)/shard_map/pallas_call | solution.py:122
  43.4 1.3 add_bitcast_fusion.1
  44.8 3.4 %collective-permute-start = (f32[2,256]{1,0:T(2,128)S(1)}, f32[2,256]{1,0:T(2,128)S(1)}, u32[]{:S(2)}, u32[]{:S(2)}) collective-permute-start(f32[2,256]{1,0:T(2,128)S(1)} %slice.470), channel_id=1, source_target_pairs={{0,4},{4,8},{8,12},{1,5},{5,9},{9,13},{2,6},{6,10},{10,14},{3,7},{... | collective-permute-start | bytes 6152 | tf_op jit(solution)/shard_map/ppermute | solution.py:28
  48.2 1.1 convolution_convert_fusion.4
  49.3 1.2 convolution_convert_fusion.3
  50.6 0.7 multiply_convert_fusion.4
  51.3 7.7 %shard_map.296 = bf16[4,128,256]{2,1,0:T(8,128)(2,1)} custom-call(bf16[128,256]{1,0:T(8,128)(2,1)} %get-tuple-element.110.refs_0_), custom_call_target="tpu_custom_call" | custom-call | tf_op jit(solution)/shard_map/pallas_call | solution.py:122
  59.0 1.9 convolution_convert_fusion.8
  60.9 9.2 %shard_map.297 = (bf16[4,128,256]{2,1,0:T(8,128)(2,1)}, bf16[4,128,512]{2,1,0:T(8,128)(2,1)}) custom-call(bf16[4,128,256]{2,1,0:T(8,128)(2,1)} %bitcast.342, bf16[4,128,512]{2,1,0:T(8,128)(2,1)} %bitcast.336), custom_call_target="tpu_custom_call" | custom-call | tf_op jit(solution)/shard_map/pallas_call | solution.py:122
  70.1 1.6 multiply_reduce_fusion.5
  71.7 5.2 %shard_map.298 = f32[4,1,128]{2,1,0:T(1,128)} custom-call(f32[1,128]{1,0:T(1,128)} %bitcast.382), custom_call_target="tpu_custom_call" | custom-call | tf_op jit(solution)/shard_map/pallas_call | solution.py:122
  77.6 0.7 multiply_convert_fusion.3.refs_0_
  78.3 9.5 %shard_map.299 = (bf16[4,128,256]{2,1,0:T(8,128)(2,1)}, bf16[4,128,640]{2,1,0:T(8,128)(2,1)}) custom-call(bf16[128,256]{1,0:T(8,128)(2,1)} %multiply_convert_fusion.3.refs_0_, bf16[4,128,640]{2,1,0:T(8,128)(2,1)} %bitcast.329), custom_call_target="tpu_custom_call" | custom-call | tf_op jit(solution)/shard_map/pallas_call | solution.py:122
  87.8 2.6 convolution_convert_fusion
  90.4 1.6 convolution_convert_fusion.1
  92.2 25.6 %shard_map.300 = (bf16[4,128,1152]{2,1,0:T(8,128)(2,1)}, bf16[4,128,1152]{2,1,0:T(8,128)(2,1)}) custom-call(bf16[4,128,1152]{2,1,0:T(8,128)(2,1)} %bitcast.324, bf16[4,128,1152]{2,1,0:T(8,128)(2,1)} %bitcast.323), custom_call_target="tpu_custom_call" | custom-call | tf_op jit(solution)/shard_map/pallas_call | solution.py:122
  117.8 2.3 multiply_convert_fusion.refs_1_
  120.1 2.6 fusion.29
  122.7 27.3 %shard_map.301 = (bf16[4,128,1152]{2,1,0:T(8,128)(2,1)}, bf16[4,128,1152]{2,1,0:T(8,128)(2,1)}) custom-call(bf16[128,1152]{1,0:T(8,128)(2,1)} %get-tuple-element.113.refs_0_, bf16[128,1152]{1,0:T(8,128)(2,1)} %multiply_convert_fusion.refs_1_), custom_call_target="tpu_custom_call" | custom-call | tf_op jit(solution)/shard_map/pallas_call | solution.py:122
  150.1 2.8 %fusion = bf16[1152,256]{1,0:T(8,128)(2,1)} fusion(bf16[4,128,1152]{2,1,0:T(8,128)(2,1)} %get-tuple-element.67, bf16[4,128,256]{2,1,0:T(8,128)(2,1)} %get-tuple-element.62), kind=kOutput, calls=%fused_computation.5 | convolution fusion | flops 302284800 | bytes 2031616 | tf_op jit(solution)/shard_map/dot_general | solution.py:36
  153.8 0.7 fusion.82
  154.5 1.3 fusion.1
  155.9 1.2 fusion.4
  157.1 10.1 %shard_map.302 = (bf16[4,128,256]{2,1,0:T(8,128)(2,1)}, bf16[4,64,1152]{2,1,0:T(8,128)(2,1)}) custom-call(bf16[4,128,256]{2,1,0:T(8,128)(2,1)} %bitcast.341, bf16[64,1152]{1,0:T(8,128)(2,1)} %get-tuple-element.123.refs_1_), custom_call_target="tpu_custom_call" | custom-call | tf_op jit(solution)/shard_map/pallas_call | solution.py:122
  167.2 2.0 constant_dynamic-update-slice_fusion.1
  169.8 5.5 %shard_map.303 = f32[4,1,128]{2,1,0:T(1,128)} custom-call(f32[1,128]{1,0:T(1,128)} %bitcast.383), custom_call_target="tpu_custom_call" | custom-call | tf_op jit(solution)/shard_map/pallas_call | solution.py:122
  176.0 0.8 fusion.81
  176.8 9.3 %shard_map.304 = (bf16[4,128,256]{2,1,0:T(8,128)(2,1)}, bf16[4,64,1152]{2,1,0:T(8,128)(2,1)}) custom-call(bf16[128,256]{1,0:T(8,128)(2,1)} %get-tuple-element.106.refs_0_, bf16[64,1152]{1,0:T(8,128)(2,1)} %get-tuple-element.122.refs_1_), custom_call_target="tpu_custom_call" | custom-call | tf_op jit(solution)/shard_map/pallas_call | solution.py:122
  186.1 1.9 constant_dynamic-update-slice_fusion
  188.0 2.7 fusion.2
  190.7 0.9 fusion.13
  191.6 1.0 convolution_convert_fusion.7
  192.6 6.8 %shard_map.305 = bf16[4,128,256]{2,1,0:T(8,128)(2,1)} custom-call(bf16[4,128,256]{2,1,0:T(8,128)(2,1)} %bitcast.347), custom_call_target="tpu_custom_call" | custom-call | tf_op jit(solution)/shard_map/pallas_call | solution.py:122
  199.4 2.5 convolution_convert_fusion.6
  202.1 1.5 collective-permute-start.1
  204.2 3.4 %collective-permute-done.1 = f32[2,256]{1,0:T(2,128)S(1)} collective-permute-done((f32[2,256]{1,0:T(2,128)S(1)}, f32[2,256]{1,0:T(2,128)S(1)}, u32[]{:S(2)}, u32[]{:S(2)}) %collective-permute-start.1) | collective-permute-done | bytes 2080 | tf_op jit(solution)/shard_map/ppermute | solution.py:28
  208.3 15.2 %shard_map.306 = (bf16[4,128,768]{2,1,0:T(8,128)(2,1)}, bf16[4,128,256]{2,1,0:T(8,128)(2,1)}, f32[8,3,256]{2,1,0:T(4,128)}) custom-call(bf16[128,768]{1,0:T(8,128)(2,1)} %pad_maximum_fusion.1.refs_0_, bf16[4,128,256]{2,1,0:T(8,128)(2,1)} %bitcast.361, f32[3,256]{1,0:T(4,128)} %pad_maximum_fusion.4.refs_2_), custom_call_target="tpu_custom_call" | custom-call | tf_op jit(solution)/shard_map/pallas_call | solution.py:122
  223.6 1.6 fusion.3
  225.4 0.9 copy.44
  226.3 1.1 convolution_convert_fusion.5
  227.4 10.5 %shard_map.307 = (bf16[4,128,256]{2,1,0:T(8,128)(2,1)}, bf16[2,3,256,128]{3,2,1,0:T(8,128)(2,1)}, bf16[2,128,256]{2,1,0:T(8,128)(2,1)}, bf16[2,576,256]{2,1,0:T(...) custom-call(bf16[4,128,256]{2,1,0:T(8,128)(2,1)} %bitcast.345, ...), custom_call_target="tpu_custom_call" | custom-call | tf_op jit(solution)/shard_map/pallas_call | solution.py:122
  237.9 1.0 multiply_bitcast_fusion.1
  238.8 2.4 fusion.56
  241.8 6.6 %shard_map.308 = (f32[4,1,128]{2,1,0:T(1,128)}, f32[8,2,256]{2,1,0:T(2,128)}) custom-call(f32[1,128]{1,0:T(1,128)} %bitcast.381, f32[2,256]{1,0:T(2,128)} %pad_maximum_fusion.5.refs_1_), custom_call_target="tpu_custom_call" | custom-call | tf_op jit(solution)/shard_map/pallas_call | solution.py:122
  248.4 0.7 multiply_bitcast_fusion.2
  249.4 1.0 copy-done.4
  250.4 1.5 multiply_subtract_fusion
  253.9 1.2 add_select_fusion.1
  255.7 1.9 copy-done
  257.9 1.9 multiply_multiply_fusion
  259.8 1.8 add_select_fusion
  261.7 0.8 add_select_fusion.3
  263.8 1.1 multiply_multiply_fusion.3
  264.8 1.1 add_select_fusion.2
  265.9 0.8 multiply_add_fusion
  (144 shorter events, 13.0 us)
Async XLA Ops:
  0.7 2.3 copy-start.9
  2.1 1.6 copy-start.15
  2.1 2.3 copy-start.40
  2.1 3.0 %copy-start.50 = (f32[3,128]{1,0:T(4,128)S(1)}, f32[3,128]{1,0:T(4,128)}, u32[]{:S(2)}) copy-start(f32[3,128]{1,0:T(4,128)} %param.17) | copy-start | bytes 4612
  2.1 3.5 %copy-start.5 = (f32[128,256]{1,0:T(8,128)S(1)}, f32[128,256]{1,0:T(8,128)}, u32[]{:S(2)}) copy-start(f32[128,256]{1,0:T(8,128)} %param.14) | copy-start | bytes 393220
  3.7 11.7 %copy-start.48 = (f32[2,256]{1,0:T(2,128)S(1)}, f32[2,256]{1,0:T(2,128)}, u32[]{:S(2)}) copy-start(f32[2,256]{1,0:T(2,128)} %param.21) | copy-start | bytes 6148
  6.3 21.3 %copy-start.38 = (f32[128,256]{1,0:T(8,128)S(1)}, f32[128,256]{1,0:T(8,128)}, u32[]{:S(2)}) copy-start(f32[128,256]{1,0:T(8,128)} %param.15) | copy-start | bytes 393220
  30.4 17.7 %copy-start.30 = (bf16[2,576,256]{2,1,0:T(8,128)(2,1)S(1)}, bf16[2,576,256]{2,1,0:T(8,128)(2,1)}, u32[]{:S(2)}) copy-start(bf16[2,576,256]{2,1,0:T(8,128)(2,1)} %get-tuple-element.58) | copy-start | bytes 1769476
  43.3 4.8 %copy-start.20 = (bf16[4,128,256]{2,1,0:T(8,128)(2,1)S(1)}, bf16[4,128,256]{2,1,0:T(8,128)(2,1)}, u32[]{:S(2)}) copy-start(bf16[4,128,256]{2,1,0:T(8,128)(2,1)} %get-tuple-element.57) | copy-start | bytes 786436
  44.7 5.8 %copy-start.51 = (bf16[2,3,128]{2,1,0:T(4,128)(2,1)S(1)}, bf16[2,3,128]{2,1,0:T(4,128)(2,1)}, u32[]{:S(2)}) copy-start(bf16[2,3,128]{2,1,0:T(4,128)(2,1)} %get-tuple-element.55) | copy-start | bytes 4612
  44.7 5.8 %copy-start.47 = (f32[2,3,128]{2,0,1:T(2,128)S(1)}, f32[2,3,128]{2,0,1:T(2,128)}, u32[]{:S(2)}) copy-start(f32[2,3,128]{2,0,1:T(2,128)} %param.23) | copy-start | bytes 9220
  44.8 5.8 %collective-permute-start = (f32[2,256]{1,0:T(2,128)S(1)}, f32[2,256]{1,0:T(2,128)S(1)}, u32[]{:S(2)}, u32[]{:S(2)}) collective-permute-start(f32[2,256]{1,0:T(2,128)S(1)} %slice.470), channel_id=1, source_target_pairs={{0,4},{4,8},{8,12},{1,5},{5,9},{9,13},{2,6},{6,10},{10,14},{3,7},{... | collective-permute-start | bytes 6152 | tf_op jit(solution)/shard_map/ppermute | solution.py:28
  49.3 9.8 %copy-start.34 = (bf16[2,128,256]{2,1,0:T(8,128)(2,1)S(1)}, bf16[2,128,256]{2,1,0:T(8,128)(2,1)}, u32[]{:S(2)}) copy-start(bf16[2,128,256]{2,1,0:T(8,128)(2,1)} %get-tuple-element.56) | copy-start | bytes 393220
  60.9 26.9 %copy-start.11 = (bf16[2,576,256]{2,1,0:T(8,128)(2,1)S(1)}, bf16[2,576,256]{2,1,0:T(8,128)(2,1)}, u32[]{:S(2)}) copy-start(bf16[2,576,256]{2,1,0:T(8,128)(2,1)} %get-tuple-element.64) | copy-start | bytes 1769476
  87.8 2.6 copy-start.12
  87.8 2.6 copy-start.27
  90.4 1.6 copy-start.29
  90.4 1.6 copy-start.35
  117.8 2.3 copy-start.3
  150.0 2.8 %copy-start.13 = (bf16[2,576,256]{2,1,0:T(8,128)(2,1)S(1)}, bf16[2,576,256]{2,1,0:T(8,128)(2,1)}, u32[]{:S(2)}) copy-start(bf16[2,576,256]{2,1,0:T(8,128)(2,1)} %get-tuple-element.63) | copy-start | bytes 1769476
  150.0 2.8 %copy-start.19 = (bf16[4,128,1152]{2,1,0:T(8,128)(2,1)S(1)}, bf16[4,128,1152]{2,1,0:T(8,128)(2,1)}, u32[]{:S(2)}) copy-start(bf16[4,128,1152]{2,1,0:T(8,128)(2,1)} %get-tuple-element.67) | copy-start | bytes 3538948
  152.8 1.0 copy-start.17
  152.8 1.7 copy-start.18
  152.8 1.7 copy-start.28
  157.1 18.9 %copy-start.39 = (f32[128,256]{1,0:T(8,128)S(1)}, f32[128,256]{1,0:T(8,128)}, u32[]{:S(2)}) copy-start(f32[128,256]{1,0:T(8,128)} %param.15) | copy-start | bytes 393220
  167.2 2.0 copy-start.24
  169.1 18.9 %copy-start.21 = (bf16[4,128,256]{2,1,0:T(8,128)(2,1)S(1)}, bf16[4,128,256]{2,1,0:T(8,128)(2,1)}, u32[]{:S(2)}) copy-start(bf16[4,128,256]{2,1,0:T(8,128)(2,1)} %get-tuple-element.57) | copy-start | bytes 786436
  188.0 2.7 %copy-start.10 = (bf16[4,128,256]{2,1,0:T(8,128)(2,1)S(1)}, bf16[4,128,256]{2,1,0:T(8,128)(2,1)}, u32[]{:S(2)}) copy-start(bf16[4,128,256]{2,1,0:T(8,128)(2,1)} %shard_map.296) | copy-start | bytes 786436
  188.0 2.7 %copy-start.22 = (bf16[4,128,256]{2,1,0:T(8,128)(2,1)S(1)}, bf16[4,128,256]{2,1,0:T(8,128)(2,1)}, u32[]{:S(2)}) copy-start(bf16[4,128,256]{2,1,0:T(8,128)(2,1)} %get-tuple-element.70) | copy-start | bytes 786436
  190.7 8.7 %copy-start.31 = (bf16[2,576,256]{2,1,0:T(8,128)(2,1)S(1)}, bf16[2,576,256]{2,1,0:T(8,128)(2,1)}, u32[]{:S(2)}) copy-start(bf16[2,576,256]{2,1,0:T(8,128)(2,1)} %get-tuple-element.58) | copy-start | bytes 1769476
  199.4 2.6 copy-start.25
  199.4 2.6 copy-start.37
  202.0 21.6 %copy-start.14 = (bf16[4,128,256]{2,1,0:T(8,128)(2,1)S(1)}, bf16[4,128,256]{2,1,0:T(8,128)(2,1)}, u32[]{:S(2)}) copy-start(bf16[4,128,256]{2,1,0:T(8,128)(2,1)} %shard_map.294) | copy-start | bytes 786436
  202.1 5.5 %collective-permute-start.1 = (f32[2,256]{1,0:T(2,128)S(1)}, f32[2,256]{1,0:T(2,128)S(1)}, u32[]{:S(2)}, u32[]{:S(2)}) collective-permute-start(f32[2,256]{1,0:T(2,128)S(1)} %slice.479), channel_id=1, source_target_pairs={{4,0},{8,4},{12,8},{5,1},{9,5},{13,9},{6,2},{10,6},{14,10},{7,3},{... | collective-permute-start | bytes 6152 | tf_op jit(solution)/shard_map/ppermute | solution.py:28
  223.6 2.7 %copy-start.7 = (bf16[4,128,768]{2,1,0:T(8,128)(2,1)S(1)}, bf16[4,128,768]{2,1,0:T(8,128)(2,1)}, u32[]{:S(2)}) copy-start(bf16[4,128,768]{2,1,0:T(8,128)(2,1)} %get-tuple-element.74) | copy-start | bytes 2359300
  227.4 11.5 %copy-start.26 = (f32[2,128,256]{2,1,0:T(8,128)S(1)}, f32[2,128,256]{2,1,0:T(8,128)}, u32[]{:S(2)}) copy-start(f32[2,128,256]{2,1,0:T(8,128)} %param.24) | copy-start | bytes 786436
  227.4 11.5 %copy-start.41 = (f32[128,256]{1,0:T(8,128)S(1)}, f32[128,256]{1,0:T(8,128)}, u32[]{:S(2)}) copy-start(f32[128,256]{1,0:T(8,128)} %param.18) | copy-start | bytes 393220
  237.8 11.3 %copy-start.8 = (bf16[2,576,256]{2,1,0:T(8,128)(2,1)S(1)}, bf16[2,576,256]{2,1,0:T(8,128)(2,1)}, u32[]{:S(2)}) copy-start(bf16[2,576,256]{2,1,0:T(8,128)(2,1)} %get-tuple-element.82) | copy-start | bytes 1769476
  241.2 8.1 %copy-start.44 = (f32[8,3,256]{2,1,0:T(4,128)S(1)}, f32[8,3,256]{2,1,0:T(4,128)}, u32[]{:S(2)}) copy-start(f32[8,3,256]{2,1,0:T(4,128)} %get-tuple-element.78) | copy-start | bytes 73732
  241.2 8.1 %copy-start.42 = (bf16[2,3,256,128]{3,2,1,0:T(8,128)(2,1)S(1)}, bf16[2,3,256,128]{3,2,1,0:T(8,128)(2,1)}, u32[]{:S(2)}) copy-start(bf16[2,3,256,128]{3,2,1,0:T(8,128)(2,1)} %get-tuple-element.77) | copy-start | bytes 1179652
  249.1 2.8 %copy-start.45 = (f32[1,2,256]{2,1,0:T(2,128)}, f32[1,2,256]{2,1,0:T(2,128)S(1)}, u32[]{:S(2)}) copy-start(f32[1,2,256]{2,1,0:T(2,128)S(1)} %get-tuple-element.92) | copy-start | bytes 6148
  249.2 1.3 copy-start.4
  250.4 13.3 %copy-start.16 = (f32[256,3,128]{2,0,1:T(8,128)}, f32[256,3,128]{2,0,1:T(8,128)S(1)}, u32[]{:S(2)}) copy-start(f32[256,3,128]{2,0,1:T(8,128)S(1)} %get-tuple-element.98) | copy-start | bytes 1179652
  250.4 1.5 copy-start.52
  250.4 1.5 copy-start.46
  250.4 2.1 copy-start.43
  253.9 1.3 copy-start.32
  253.9 1.5 copy-start.33
  255.5 2.1 copy-start
  255.5 2.4 copy-start.2
  255.7 4.1 %copy-start.1 = (f32[256,2,576]{0,2,1:T(8,128)}, f32[256,2,576]{0,2,1:T(8,128)S(1)}, u32[]{:S(2)}) copy-start(f32[256,2,576]{0,2,1:T(8,128)S(1)} %get-tuple-element.94) | copy-start | bytes 3538948
  261.7 2.1 copy-start.6
  262.5 2.3 copy-start.49
  264.8 1.1 copy-start.23
  264.8 1.1 copy-start.36

commit v3 on v2

--- a/solution.py
+++ b/solution.py
@@ -20,12 +20,6 @@
 matrix_rate = 0.01
 small_rate = 0.1
 decay_rate = 0.1
-
-
-def shifted(x, axis, by):
-    devices = lax.axis_size(axis)
-    pairs = [(i, i + by) for i in range(devices) if 0 <= i + by < devices]
-    return lax.ppermute(x, axis, pairs)
 
 
 def plain_product(left_side, right_side):
@@ -229,11 +223,15 @@
     inverse_one = inverse_rms(added(stats)[0])
     normed_one = (block_input * inverse_one * gain_one).astype(low)
     gathered_one = flat_rows(exchange(ids, gather(COL, normed_one))[0])
-    projected, gathered_cot = exchange(
-        ids,
-        swap(ROW, plain_product(gathered_one, proj_matrix)),
+    projected_item = swap(ROW, plain_product(gathered_one, proj_matrix))
+    before_blocks = jnp.roll(projected_item[1][:, -history:], 1, axis=0)
+    projected, before, gathered_cot = exchange(
+        ids,
+        projected_item,
+        (ROW, before_blocks, False),
         gather(COL, out_cot.astype(low)),
     )
+    before = added(before)
     projected = added(projected)
     gathered_cot = flat_rows(gathered_cot)
     inner_rows = projected.shape[0]
@@ -242,13 +240,20 @@
     gate_c = projected[:, channels : 2 * channels]
     values_x = projected[:, 2 * channels :]
     mixed_input = gate_b * values_x
-    left_rim = shifted(mixed_input[inner_rows - history :], "row", 1)
+    row_index = lax.axis_index("row")
+    before_mixed = before[:, :channels] * before[:, 2 * channels :]
+    left_rim = jnp.where(row_index > 0, before_mixed, 0.0)
     padded = jnp.concatenate([left_rim, mixed_input], axis=0)
     convolved = conv_taps[0] * padded[0:inner_rows]
     for offset in range(1, KERNEL):
         convolved = convolved + conv_taps[offset] * padded[offset : offset + inner_rows]
     gated = (gate_c * convolved).astype(low)
-    gathered_gated = flat_rows(exchange(ids, gather(ROW, gated))[0])
+    gathered_gated, gate_rims = exchange(ids, gather(ROW, gated), gather(ROW, gate_c[:history]))
+    gathered_gated = flat_rows(gathered_gated)
+    row_devices = lax.axis_size("row")
+    gate_after = lax.dynamic_index_in_dim(
+        gate_rims, lax.rem(row_index + 1, row_devices), 0, keepdims=False
+    )
     mixer_out, d_hidden_a = exchange(
         ids,
         swap(COL, plain_product(gathered_gated, wide_mixer)),
@@ -278,34 +283,40 @@
     hidden = (swish_gate * lifted).astype(low)
     d_gate = d_hidden * lifted * sigmoid_gate * (1.0 + gate_pre * (1.0 - sigmoid_gate))
     d_lifted = d_hidden * swish_gate
-    gathered_dgate, gathered_dlift = map(
-        flat_rows,
-        exchange(ids, gather(ROW, d_gate.astype(low)), gather(ROW, d_lifted.astype(low))),
-    )
-    hidden_half = inner_rows // 2
-    d_normed_two, hidden_a = exchange(
+    d_gate = d_gate.astype(low)
+    d_lifted = d_lifted.astype(low)
+    unit_sums = jnp.sum(d_gate * gate_pre + d_lifted * lifted, axis=1)[None, :]
+    gathered_dgate, gathered_dlift, unit_sums = exchange(
+        ids, gather(ROW, d_gate), gather(ROW, d_lifted), gather(ROW, unit_sums)
+    )
+    gathered_dgate, gathered_dlift = map(flat_rows, (gathered_dgate, gathered_dlift))
+    token_sums = unit_sums.reshape(lax.axis_size("col"), 1, -1)
+    d_normed_two, hidden_a, token_sums = exchange(
         ids,
         swap(
             COL,
             plain_product(gathered_dgate, wide_gate) + plain_product(gathered_dlift, wide_lift),
         ),
-        gather(ROW, hidden[:hidden_half]),
+        gather(ROW, hidden[:, :half]),
+        (COL, token_sums, False),
     )
     d_normed_two = added(d_normed_two)
-    (stats,) = exchange(ids, gather(ROW, back_sums(residual_two, gain_two, d_normed_two)))
     d_residual = out_cot + norm_back(
-        residual_two, inverse_two, gain_two, d_normed_two, added(stats)[0]
+        residual_two, inverse_two, gain_two, d_normed_two, added(token_sums)[0] / inverse_two[:, 0]
     )
     gathered_dres, hidden_b = exchange(
-        ids, gather(COL, d_residual.astype(low)), gather(ROW, hidden[hidden_half:])
+        ids, gather(COL, d_residual.astype(low)), gather(ROW, hidden[:, half:])
     )
     gathered_dres = flat_rows(gathered_dres)
-    gathered_hidden = flat_rows(jnp.concatenate([hidden_a, hidden_b], axis=1))
-    (d_gated,) = exchange(ids, swap(ROW, contract_cols(gathered_dres, wide_mixer)))
-    d_gated = added(d_gated)
+    hidden_a, hidden_b = map(flat_rows, (hidden_a, hidden_b))
+    d_gated_item = swap(ROW, contract_cols(gathered_dres, wide_mixer))
+    after_blocks = jnp.roll(d_gated_item[1][:, :history], -1, axis=0)
+    d_gated, d_gated_after = map(
+        added, exchange(ids, d_gated_item, (ROW, after_blocks, False))
+    )
     d_convolved = d_gated * gate_c
     d_gate_c = d_gated * convolved
-    next_rim = shifted(d_convolved[:history], "row", -1)
+    next_rim = jnp.where(row_index < row_devices - 1, d_gated_after * gate_after, 0.0)
     extended = jnp.concatenate([d_convolved, next_rim], axis=0)
     d_mixed = conv_taps[history] * extended[0:inner_rows]
     for offset in range(1, KERNEL):
@@ -322,11 +333,21 @@
     gathered_dproj, ffn_out, conv_parts = exchange(
         ids,
         gather(ROW, d_projected),
-        swap(COL, plain_product(gathered_hidden, wide_down)),
+        swap(
+            COL,
+            plain_product(hidden_a, wide_down[:half]) + plain_product(hidden_b, wide_down[half:]),
+        ),
         gather(("dp", "row"), conv_part),
     )
     gathered_dproj = flat_rows(gathered_dproj)
     block_output = residual_two + added(ffn_out)
+    down_part = jnp.concatenate(
+        [
+            contract_rows(hidden_a, gathered_cot).astype(low),
+            contract_rows(hidden_b, gathered_cot).astype(low),
+        ],
+        axis=0,
+    )
     proj_part = contract_rows(gathered_one, gathered_dproj).astype(low)
     proj_part = proj_part.reshape(width_local, 3, replicas, shard_width).transpose(2, 1, 0, 3)
     d_normed_one, proj_grad, mixer_grad, up_grad_gate, up_grad_lift, down_grad = map(
@@ -338,7 +359,7 @@
             swap(DP, contract_rows(gathered_gated, gathered_dres)),
             swap(DP, contract_rows(gathered_dgate, gathered_two)),
             swap(DP, contract_rows(gathered_dlift, gathered_two)),
-            swap(DP, contract_rows(gathered_hidden, gathered_cot)),
+            swap(DP, down_part),
         ),
     )
     gains_part = jnp.stack(

time: 267 us -> 257 us (0.963)
  starting transfers between devices: 4.84 us -> 0 us
  waiting for transfers between devices: 3.4 us -> 0 us
  other arithmetic: 38.9 us -> 42.3 us
  local copies, waits for them, and re-layouts: 11.9 us -> 8.95 us
    ppermute x2 -> x0, starting transfers between devices: 4.84 us -> none  [shifted(): return lax.ppermute(x, axis, pairs)]
    ppermute x2 -> x0, waiting for transfers between devices: 3.4 us -> none  [shifted(): return lax.ppermute(x, axis, pairs)]
    dot_general x5 -> x6, matrix products: 9.29 us -> 7.01 us  [contract_rows(): lax.dot_general(left_side, right_side, (((0,), (0,)), ((), ())), preferre...]
    unnamed x107 -> x118, local copies, waits for them, and re-layouts: 6.07 us -> 3.85 us
    dot_general x5 -> x6, matrix products: 8.35 us -> 8.74 us  [plain_product(): return jnp.dot(left_side, right_side, preferred_element_type=jnp.float32)]
    pallas_call x16 -> x15, Pallas kernels: 180 us -> 180 us  [exchange(): pl.pallas_call(kernel, out_shape=[jax.ShapeDtypeStruct((devices[axes],) +...]
  transfers between devices with their start and end apart: 2 -> 0, of which waited for: 1 -> 0; matrix products, arithmetic and copies ran while one was open for 1% -> 0% of each run, Pallas kernels for 0% -> 0%
where the time goes in v3:
time: 257 us
  Pallas kernels  180 us (70%)
  other arithmetic  42.3 us (16%)
  matrix products  23.6 us (9%)
  local copies, waits for them, and re-layouts  8.95 us (3%)
    pallas_call x15, Pallas kernels, exchange(): pl.pallas_call(kernel, out_shape=[jax.ShapeDtypeStruct((devices[axes],) +...  180 us
    dot_general x6, matrix products, plain_product(): return jnp.dot(left_side, right_side, preferred_element_type=jnp.float32)  8.74 us
    dot_general x6, matrix products, contract_cols(): lax.dot_general(left_side, right_side, (((1,), (1,)), ((), ())), preferre...  7.82 us
    dot_general x6, matrix products, contract_rows(): lax.dot_general(left_side, right_side, (((0,), (0,)), ((), ())), preferre...  7.01 us
    select_n x6, other arithmetic, adam_step(): jnp.where(is_first, beta_first * moments + (1.0 - beta_first) * gradient[...  6.25 us

profile of v3, /device:TPU:0, one launch (start us, length us, event | category | flops | bytes accessed | tf_op | source)
XLA Modules:
  0.0 256.6 jit_solution(7116183977674964111)
XLA Ops:
  0.7 1.4 convert_bitcast_fusion
  2.1 0.8 slice_bitcast_fusion
  3.0 0.7 convert_element_type.349.refs_6_
  3.7 0.7 convert_bitcast_fusion.1.refs_1_
  6.3 8.4 %shard_map.293 = (f32[4,1,128]{2,1,0:T(1,128)}, bf16[2,3,256,128]{3,2,1,0:T(8,128)(2,1)}, bf16[2,3,128]{2,1,0:T(4,128)(2,1)}, bf16[2,128,256]{2,1,0:T(8,128)(2,1...) custom-call(f32[1,128]{1,0:T(1,128)} %bitcast.409, ...), custom_call_target="tpu_custom_call" | custom-call | tf_op jit(solution)/shard_map/pallas_call | solution.py:116
  14.6 0.7 rsqrt_bitcast_fusion.1
  15.4 0.7 multiply_convert_fusion.5.refs_0_
  16.1 10.2 %shard_map.294 = bf16[4,128,256]{2,1,0:T(8,128)(2,1)} custom-call(bf16[128,256]{1,0:T(8,128)(2,1)} %multiply_convert_fusion.5.refs_0_), custom_call_target="tpu_custom_call" | custom-call | tf_op jit(solution)/shard_map/pallas_call | solution.py:116
  26.3 1.2 copy.42
  27.5 1.4 convolution_convert_fusion.2
  28.9 0.7 pad_maximum_fusion.5.refs_1_
  30.3 13.5 %shard_map.295 = (bf16[4,128,768]{2,1,0:T(8,128)(2,1)}, bf16[4,2,768]{2,1,0:T(2,128)(2,1)}, bf16[4,128,256]{2,1,0:T(8,128)(2,1)}) custom-call(bf16[4,128,768]{2,1,0:T(8,128)(2,1)} %bitcast.353, bf16[4,2,768]{2,1,0:T(2,128)(2,1)} %pad_maximum_fusion.5.refs_1_, bf16[128,256]{1,0:T(8,128)(2,1)} %convert_element_type.352.refs_2_), custom_call_target="tpu_custom_call" | custom-call | tf_op jit(solution)/shard_map/pallas_call | solution.py:116
  43.9 1.4 add_bitcast_fusion.1
  45.4 0.7 multiply_convert_fusion.4
  46.7 7.4 %shard_map.296 = (bf16[4,128,256]{2,1,0:T(8,128)(2,1)}, f32[4,2,256]{2,1,0:T(2,128)}) custom-call(bf16[128,256]{1,0:T(8,128)(2,1)} %get-tuple-element.129.refs_0_, f32[2,256]{1,0:T(2,128)} %slice.543.refs_1_), custom_call_target="tpu_custom_call" | custom-call | tf_op jit(solution)/shard_map/pallas_call | solution.py:116
  54.2 1.9 convolution_convert_fusion.7
  56.0 1.1 convolution_convert_fusion.4
  57.2 9.3 %shard_map.297 = (bf16[4,128,256]{2,1,0:T(8,128)(2,1)}, bf16[4,128,512]{2,1,0:T(8,128)(2,1)}) custom-call(bf16[4,128,256]{2,1,0:T(8,128)(2,1)} %bitcast.376, bf16[4,128,512]{2,1,0:T(8,128)(2,1)} %bitcast.366), custom_call_target="tpu_custom_call" | custom-call | tf_op jit(solution)/shard_map/pallas_call | solution.py:116
  66.4 1.6 multiply_reduce_fusion.4
  68.0 5.9 %shard_map.298 = f32[4,1,128]{2,1,0:T(1,128)} custom-call(f32[1,128]{1,0:T(1,128)} %bitcast.411), custom_call_target="tpu_custom_call" | custom-call | tf_op jit(solution)/shard_map/pallas_call | solution.py:116
  74.5 0.7 multiply_convert_fusion.3.refs_0_
  75.3 1.2 convolution_convert_fusion.3
  76.5 10.4 %shard_map.299 = (bf16[4,128,256]{2,1,0:T(8,128)(2,1)}, bf16[4,128,640]{2,1,0:T(8,128)(2,1)}) custom-call(bf16[128,256]{1,0:T(8,128)(2,1)} %multiply_convert_fusion.3.refs_0_, bf16[4,128,640]{2,1,0:T(8,128)(2,1)} %bitcast.355), custom_call_target="tpu_custom_call" | custom-call | tf_op jit(solution)/shard_map/pallas_call | solution.py:116
  86.9 2.6 %convolution_convert_fusion = bf16[512,1152]{1,0:T(8,128)(2,1)} fusion(bf16[512,256]{1,0:T(8,128)(2,1)} %bitcast.382, bf16[1152,256]{1,0:T(8,128)(2,1)S(1)} %bitcast.361), kind=kOutput, calls=%fused_computation | convolution fusion | flops 302579712 | bytes 2031616 | tf_op jit(solution)/shard_map/dot_general | solution.py:36
  89.5 1.6 convolution_convert_fusion.1
  91.1 27.7 %shard_map.300 = (bf16[4,128,1152]{2,1,0:T(8,128)(2,1)}, bf16[4,128,1152]{2,1,0:T(8,128)(2,1)}) custom-call(bf16[4,128,1152]{2,1,0:T(8,128)(2,1)} %bitcast.348, bf16[4,128,1152]{2,1,0:T(8,128)(2,1)} %bitcast.347), custom_call_target="tpu_custom_call" | custom-call | tf_op jit(solution)/shard_map/pallas_call | solution.py:116
  118.8 2.1 fusion.33
  121.1 1.1 copy-done.2
  122.2 1.8 fusion.31
  124.0 29.4 %shard_map.301 = (bf16[4,128,1152]{2,1,0:T(8,128)(2,1)}, bf16[4,128,1152]{2,1,0:T(8,128)(2,1)}, f32[4,1,128]{2,1,0:T(1,128)}) custom-call(bf16[128,1152]{1,0:T(8,128)(2,1)} %get-tuple-element.124.refs_0_, bf16[128,1152]{1,0:T(8,128)(2,1)} %get-tuple-element.123.refs_1_, f32[1,128]{1,0:T(1,128)} %bitcast.412), custom_call_target="tpu_custom_call" | custom-call | tf_op jit(solution)/shard_map/pallas_call | solution.py:116
  153.4 1.9 fusion.98
  155.3 1.2 fusion.4
  157.2 9.8 %shard_map.302 = (bf16[4,128,256]{2,1,0:T(8,128)(2,1)}, bf16[4,128,512]{2,1,0:T(8,128)(2,1)}, f32[4,1,128]{2,1,0:T(1,128)}) custom-call(bf16[4,128,256]{2,1,0:T(8,128)(2,1)} %bitcast.375, bf16[128,512]{1,0:T(8,128)(2,1)} %slice.546.refs_1_, f32[4,1,128]{2,1,0:T(1,128)} %get-tuple-element.78.refs_2_), custom_call_target="tpu_custom_call" | custom-call | tf_op jit(solution)/shard_map/pallas_call | solution.py:116
  166.9 0.7 multiply_bitcast_fusion.3
  167.6 1.7 fusion.92
  170.1 9.5 %shard_map.303 = (bf16[4,128,256]{2,1,0:T(8,128)(2,1)}, bf16[4,128,640]{2,1,0:T(8,128)(2,1)}) custom-call(bf16[128,256]{1,0:T(8,128)(2,1)} %get-tuple-element.118.refs_0_, bf16[128,640]{1,0:T(8,128)(2,1)} %slice.547.refs_1_), custom_call_target="tpu_custom_call" | custom-call | tf_op jit(solution)/shard_map/pallas_call | solution.py:116
  179.6 1.5 fusion.3
  181.5 0.9 pad_maximum_fusion.1
  182.4 1.3 fusion.1
  183.8 1.3 fusion
  185.1 0.9 fusion.15
  187.0 6.9 %shard_map.304 = (bf16[4,128,256]{2,1,0:T(8,128)(2,1)}, bf16[4,2,256]{2,1,0:T(2,128)(2,1)}) custom-call(bf16[4,128,256]{2,1,0:T(8,128)(2,1)} %bitcast.373, bf16[4,2,256]{2,1,0:T(2,128)(2,1)} %pad_maximum_fusion.6.refs_1_), custom_call_target="tpu_custom_call" | custom-call | tf_op jit(solution)/shard_map/pallas_call | solution.py:116
  194.0 1.0 multiply_reduce_fusion.3
  195.6 1.3 fusion.45
  197.0 1.1 fusion.5
  198.1 0.7 select_bitcast_fusion
  199.6 14.3 %shard_map.305 = (bf16[4,128,768]{2,1,0:T(8,128)(2,1)}, bf16[4,128,256]{2,1,0:T(8,128)(2,1)}, f32[8,3,256]{2,1,0:T(4,128)}) custom-call(bf16[128,768]{1,0:T(8,128)(2,1)} %pad_maximum_fusion.2.refs_0_, bf16[4,128,256]{2,1,0:T(8,128)(2,1)} %bitcast.374, f32[3,256]{1,0:T(4,128)} %pad_maximum_fusion.7.refs_2_), custom_call_target="tpu_custom_call" | custom-call | tf_op jit(solution)/shard_map/pallas_call | solution.py:116
  213.9 1.6 fusion.2
  215.7 0.9 copy.45
  216.6 1.1 convolution_convert_fusion.5
  217.7 10.5 %shard_map.306 = (bf16[4,128,256]{2,1,0:T(8,128)(2,1)}, bf16[2,3,256,128]{3,2,1,0:T(8,128)(2,1)}, bf16[2,128,256]{2,1,0:T(8,128)(2,1)}, bf16[2,576,256]{2,1,0:T(...) custom-call(bf16[4,128,256]{2,1,0:T(8,128)(2,1)} %bitcast.381, ...), custom_call_target="tpu_custom_call" | custom-call | tf_op jit(solution)/shard_map/pallas_call | solution.py:116
  228.2 2.4 fusion.63
  231.2 7.0 %shard_map.307 = (f32[4,1,128]{2,1,0:T(1,128)}, f32[8,2,256]{2,1,0:T(2,128)}) custom-call(f32[1,128]{1,0:T(1,128)} %bitcast.410, f32[2,256]{1,0:T(2,128)} %pad_maximum_fusion.8.refs_1_), custom_call_target="tpu_custom_call" | custom-call | tf_op jit(solution)/shard_map/pallas_call | solution.py:116
  238.3 0.7 multiply_bitcast_fusion.2
  239.8 1.3 add_select_fusion.1
  241.6 1.9 copy-done
  243.8 1.9 multiply_multiply_fusion
  245.7 1.8 add_select_fusion
  247.6 0.8 add_select_fusion.3
  249.7 1.1 broadcast_multiply_fusion.1
  250.8 1.1 multiply_multiply_fusion.3
  251.9 1.1 add_select_fusion.2
  253.0 1.5 multiply_subtract_fusion
  254.5 0.8 multiply_add_fusion
  (160 shorter events, 13.2 us)
Async XLA Ops:
  0.7 2.3 copy-start.10
  2.1 1.6 copy-start.16
  2.1 2.3 copy-start.45
  2.1 3.0 %copy-start.55 = (f32[3,128]{1,0:T(4,128)S(1)}, f32[3,128]{1,0:T(4,128)}, u32[]{:S(2)}) copy-start(f32[3,128]{1,0:T(4,128)} %param.17) | copy-start | bytes 4612
  2.1 3.5 %copy-start.5 = (f32[128,256]{1,0:T(8,128)S(1)}, f32[128,256]{1,0:T(8,128)}, u32[]{:S(2)}) copy-start(f32[128,256]{1,0:T(8,128)} %param.14) | copy-start | bytes 393220
  3.7 11.6 %copy-start.53 = (f32[2,256]{1,0:T(2,128)S(1)}, f32[2,256]{1,0:T(2,128)}, u32[]{:S(2)}) copy-start(f32[2,256]{1,0:T(2,128)} %param.21) | copy-start | bytes 6148
  26.3 3.4 %copy-start.42 = (f32[128,256]{1,0:T(8,128)S(1)}, f32[128,256]{1,0:T(8,128)}, u32[]{:S(2)}) copy-start(f32[128,256]{1,0:T(8,128)} %param.15) | copy-start | bytes 393220
  28.9 1.4 copy-start.6
  30.3 15.0 %copy-start.57 = (bf16[2,3,128]{2,1,0:T(4,128)(2,1)S(1)}, bf16[2,3,128]{2,1,0:T(4,128)(2,1)}, u32[]{:S(2)}) copy-start(bf16[2,3,128]{2,1,0:T(4,128)(2,1)} %get-tuple-element.62) | copy-start | bytes 4612
  43.8 1.5 copy-start.51
  43.8 10.3 %copy-start.36 = (bf16[2,128,256]{2,1,0:T(8,128)(2,1)S(1)}, bf16[2,128,256]{2,1,0:T(8,128)(2,1)}, u32[]{:S(2)}) copy-start(bf16[2,128,256]{2,1,0:T(8,128)(2,1)} %get-tuple-element.65) | copy-start | bytes 393220
  43.8 12.2 %copy-start.12 = (bf16[2,576,256]{2,1,0:T(8,128)(2,1)S(1)}, bf16[2,576,256]{2,1,0:T(8,128)(2,1)}, u32[]{:S(2)}) copy-start(bf16[2,576,256]{2,1,0:T(8,128)(2,1)} %get-tuple-element.67) | copy-start | bytes 1769476
  43.8 12.2 %copy-start.24 = (bf16[4,128,256]{2,1,0:T(8,128)(2,1)S(1)}, bf16[4,128,256]{2,1,0:T(8,128)(2,1)}, u32[]{:S(2)}) copy-start(bf16[4,128,256]{2,1,0:T(8,128)(2,1)} %get-tuple-element.66) | copy-start | bytes 786436
  45.3 21.2 %copy-start.20 = (f32[128,256]{1,0:T(8,128)}, f32[128,256]{1,0:T(8,128)S(1)}, u32[]{:S(2)}) copy-start(f32[128,256]{1,0:T(8,128)S(1)} %slice_multiply_fusion) | copy-start | bytes 393220
  68.0 18.9 %copy-start.13 = (bf16[2,576,256]{2,1,0:T(8,128)(2,1)S(1)}, bf16[2,576,256]{2,1,0:T(8,128)(2,1)}, u32[]{:S(2)}) copy-start(bf16[2,576,256]{2,1,0:T(8,128)(2,1)} %get-tuple-element.73) | copy-start | bytes 1769476
  86.9 2.6 %copy-start.14 = (bf16[2,576,256]{2,1,0:T(8,128)(2,1)S(1)}, bf16[2,576,256]{2,1,0:T(8,128)(2,1)}, u32[]{:S(2)}) copy-start(bf16[2,576,256]{2,1,0:T(8,128)(2,1)} %get-tuple-element.72) | copy-start | bytes 1769476
  86.9 2.6 %copy-start.30 = (bf16[4,128,256]{2,1,0:T(8,128)(2,1)S(1)}, bf16[4,128,256]{2,1,0:T(8,128)(2,1)}, u32[]{:S(2)}) copy-start(bf16[4,128,256]{2,1,0:T(8,128)(2,1)} %get-tuple-element.71) | copy-start | bytes 786436
  118.8 2.1 copy-start.33
  118.8 2.2 copy-start.38
  120.9 1.3 copy-start.2
  153.4 1.9 copy-start.18
  155.3 12.4 %copy-start.43 = (f32[128,256]{1,0:T(8,128)S(1)}, f32[128,256]{1,0:T(8,128)}, u32[]{:S(2)}) copy-start(f32[128,256]{1,0:T(8,128)} %param.15) | copy-start | bytes 393220
  156.5 23.1 %copy-start.25 = (bf16[4,128,256]{2,1,0:T(8,128)(2,1)S(1)}, bf16[4,128,256]{2,1,0:T(8,128)(2,1)}, u32[]{:S(2)}) copy-start(bf16[4,128,256]{2,1,0:T(8,128)(2,1)} %get-tuple-element.66) | copy-start | bytes 786436
  169.4 11.7 %copy-start.39 = (bf16[4,128,512]{2,1,0:T(8,128)(2,1)S(1)}, bf16[4,128,512]{2,1,0:T(8,128)(2,1)}, u32[]{:S(2)}) copy-start(bf16[4,128,512]{2,1,0:T(8,128)(2,1)} %get-tuple-element.85) | copy-start | bytes 1572868
  181.1 1.3 copy-start.19
  181.1 1.3 copy-start.31
  182.4 1.3 copy-start.22
  183.8 1.4 copy-start.26
  183.8 1.4 copy-start.27
  183.8 2.3 copy-start.37
  185.1 8.9 %copy-start.21 = (f32[128,256]{1,0:T(8,128)S(1)}, f32[128,256]{1,0:T(8,128)}, u32[]{:S(2)}) copy-start(f32[128,256]{1,0:T(8,128)} %copy-done.20) | copy-start | bytes 393220
  185.1 8.9 %copy-start.41 = (f32[128,256]{1,0:T(8,128)S(1)}, f32[128,256]{1,0:T(8,128)}, u32[]{:S(2)}) copy-start(f32[128,256]{1,0:T(8,128)} %get-tuple-element.130) | copy-start | bytes 393220
  186.3 0.7 copy-start.23
  187.0 10.0 %copy-start.32 = (bf16[4,128,640]{2,1,0:T(8,128)(2,1)S(1)}, bf16[4,128,640]{2,1,0:T(8,128)(2,1)}, u32[]{:S(2)}) copy-start(bf16[4,128,640]{2,1,0:T(8,128)(2,1)} %get-tuple-element.86) | copy-start | bytes 1966084
  197.0 1.1 copy-start.56
  198.1 15.8 %copy-start.15 = (bf16[4,128,256]{2,1,0:T(8,128)(2,1)S(1)}, bf16[4,128,256]{2,1,0:T(8,128)(2,1)}, u32[]{:S(2)}) copy-start(bf16[4,128,256]{2,1,0:T(8,128)(2,1)} %shard_map.294) | copy-start | bytes 786436
  213.9 2.7 %copy-start.8 = (bf16[4,128,768]{2,1,0:T(8,128)(2,1)S(1)}, bf16[4,128,768]{2,1,0:T(8,128)(2,1)}, u32[]{:S(2)}) copy-start(bf16[4,128,768]{2,1,0:T(8,128)(2,1)} %get-tuple-element.88) | copy-start | bytes 2359300
  217.7 10.5 %copy-start.29 = (f32[2,128,256]{2,1,0:T(8,128)S(1)}, f32[2,128,256]{2,1,0:T(8,128)}, u32[]{:S(2)}) copy-start(f32[2,128,256]{2,1,0:T(8,128)} %param.24) | copy-start | bytes 786436
  217.7 10.5 %copy-start.46 = (f32[128,256]{1,0:T(8,128)S(1)}, f32[128,256]{1,0:T(8,128)}, u32[]{:S(2)}) copy-start(f32[128,256]{1,0:T(8,128)} %param.18) | copy-start | bytes 393220
  228.2 10.8 %copy-start.50 = (f32[2,2,256]{2,1,0:T(2,128)S(1)}, f32[2,2,256]{2,1,0:T(2,128)}, u32[]{:S(2)}) copy-start(f32[2,2,256]{2,1,0:T(2,128)} %param.27) | copy-start | bytes 12292
  228.2 11.5 %copy-start.9 = (bf16[2,576,256]{2,1,0:T(8,128)(2,1)S(1)}, bf16[2,576,256]{2,1,0:T(8,128)(2,1)}, u32[]{:S(2)}) copy-start(bf16[2,576,256]{2,1,0:T(8,128)(2,1)} %get-tuple-element.96) | copy-start | bytes 1769476
  230.6 9.2 %copy-start.4 = (f32[2,576,256]{2,1,0:T(8,128)S(1)}, f32[2,576,256]{2,1,0:T(8,128)}, u32[]{:S(2)}) copy-start(f32[2,576,256]{2,1,0:T(8,128)} %param.26) | copy-start | bytes 3538948
  239.0 16.3 %copy-start.49 = (f32[1,2,256]{2,1,0:T(2,128)}, f32[1,2,256]{2,1,0:T(2,128)S(1)}, u32[]{:S(2)}) copy-start(f32[1,2,256]{2,1,0:T(2,128)S(1)} %get-tuple-element.104) | copy-start | bytes 6148
  239.8 1.3 copy-start.34
  239.8 1.4 copy-start.35
  241.4 2.1 copy-start
  241.4 2.4 copy-start.3
  241.6 4.1 %copy-start.1 = (f32[256,2,576]{0,2,1:T(8,128)}, f32[256,2,576]{0,2,1:T(8,128)S(1)}, u32[]{:S(2)}) copy-start(f32[256,2,576]{0,2,1:T(8,128)S(1)} %get-tuple-element.106) | copy-start | bytes 3538948
  245.7 1.8 copy-start.44
  247.6 0.8 copy-start.48
  247.6 0.9 copy-start.52
  247.6 3.3 %copy-start.7 = (f32[2,256,3,128]{3,1,2,0:T(8,128)S(1)}, f32[2,256,3,128]{3,1,2,0:T(8,128)}, u32[]{:S(2)}) copy-start(f32[2,256,3,128]{3,1,2,0:T(8,128)} %param.22) | copy-start | bytes 2359300
  248.5 3.4 %copy-start.54 = (f32[3,128]{1,0:T(4,128)}, f32[3,128]{1,0:T(4,128)S(1)}, u32[]{:S(2)}) copy-start(f32[3,128]{1,0:T(4,128)S(1)} %get-tuple-element.108) | copy-start | bytes 4612
  250.8 1.1 copy-start.17
  251.9 1.1 copy-start.11
  253.0 1.5 copy-start.58
  253.0 1.5 copy-start.28
  253.0 1.5 copy-start.40
  253.0 2.9 %copy-start.47 = (bf16[4,128,256]{2,1,0:T(8,128)(2,1)S(1)}, bf16[4,128,256]{2,1,0:T(8,128)(2,1)}, u32[]{:S(2)}) copy-start(bf16[4,128,256]{2,1,0:T(8,128)(2,1)} %get-tuple-element.87) | copy-start | bytes 786436
